TPU v7x, 128 devices: a whole 4x4x4 slice. The times are simulated.
128 devices in a mesh: depth: 4 (over y_lo, core), strips: 32 (over z, y_hi, x).
Axes of the slice: x: 4, y: 4 (y_hi: 2, y_lo: 2; y = y_hi * 2 + y_lo), z: 4, core: 2. Of those that a mesh axis runs over, the one named last changes fastest.
Arguments:
- pressure: float32 [32, 4096, 1024], P('depth', 'strips'), may hold values from -3 to 3
- texture: int32 [32, 4096, 1024], P('depth', 'strips'), may hold values from 0 to 11
- active: int32 [32, 4096, 1024], P('depth', 'strips'), may hold values 0 or 1
- rain: float32 [4096, 1024], P('strips'), may hold values from 0 to 40
- k_sat: float32 [12], replicated, may hold values from 0.05 to 2
- alpha: float32 [12], replicated, may hold values from 0.5 to 4
- theta_sat: float32 [12], replicated, may hold values from 0.35 to 0.5
- head_old: float32 [4096, 1024], P('strips', 'depth'), may hold values from -4 to 4
- cell_code: int32 [4096, 1024], P('strips', 'depth'), may hold values from 0 to 2
- section: float32 [4096, 1024], P('strips', 'depth'), may hold values from -4 to 4
Outputs:
- moisture_new: float32 [32, 4096, 1024], P('depth', 'strips')
- head: float32 [4096, 1024], P('strips', 'depth')
All inputs are finite; a program needn't handle non-finite values. No bound on the sum of `active` on one device may be relied on, other than what follows from the above.
Results may differ from a plain program's by a relative error of at most 0.00002.
Values sent between devices are 32-bit elements; how exact they have to be, the bound alone decides.
A program may use at most 128 MiB of HBM per device.

v0:
```python
import jax
import jax.numpy as jnp
from jax import lax
from jax.sharding import PartitionSpec as P

SWEEPS = 3


layer_thick = 0.05
soil_step = 0.0002
spec_yield = 0.02
leak_rate = 0.5
river_cond = 0.5
fixed_cond = 3.0


def shifted(value, axis, steps):
    count = lax.axis_size(axis)
    leading, last = (max(0, -steps), min(count, count - steps))
    return lax.ppermute(value, axis, [(source, source + steps) for source in range(leading, last)])


def with_halo(cells, sides, width):
    for axis, dim in sides:
        count = lax.axis_size(axis)
        ends = count - 1
        head = lax.slice_in_dim(cells, 0, width, axis=dim)
        tail = lax.slice_in_dim(cells, cells.shape[dim] - width, cells.shape[dim], axis=dim)
        cells = jnp.concatenate(
            [
                lax.ppermute(tail, axis, [(i, (i + 1) % count) for i in range(ends)]),
                cells,
                lax.ppermute(head, axis, [((i + 1) % count, i) for i in range(ends)]),
            ],
            axis=dim,
        )
    return cells


def lookup(texture, table):
    result = jnp.zeros(texture.shape, jnp.float32)
    for class_id in range(table.shape[0]):
        result = result + jnp.where(texture == class_id, table[class_id], jnp.float32(0.0))
    return result


def face_flux(psi_up, cond_up, psi_low, cond_low):
    return 0.5 * (cond_up + cond_low) * ((psi_up - psi_low) / layer_thick + 1.0)


def neighbour(padded, shift_a, shift_b):
    return padded[
        1 + shift_a : padded.shape[0] - 1 + shift_a, 1 + shift_b : padded.shape[1] - 1 + shift_b
    ]


def sweep(head_pad, trans_pad, base, rhs):
    centre = neighbour(trans_pad, 0, 0)
    total = base
    accum = rhs
    for shift_a, shift_b in ((1, 0), (-1, 0), (0, 1), (0, -1)):
        face = jnp.sqrt(centre * neighbour(trans_pad, shift_a, shift_b))
        accum = accum + face * neighbour(head_pad, shift_a, shift_b)
        total = total + face
    inside = total > 0.0
    return jnp.where(inside, accum / jnp.where(inside, total, 1.0), 0.0)


def shards(pressure, texture, active, rain, k_sat, alpha, theta_sat, head_old, cell_code, section):
    depth_index = lax.axis_index("depth")
    is_top = depth_index == 0
    is_bottom = depth_index == lax.axis_size("depth") - 1
    sat_cond = lookup(texture, k_sat)
    shape_par = lookup(texture, alpha)
    porous = lookup(texture, theta_sat)
    suction = jnp.minimum(pressure, 0.0)
    wetness = jnp.exp(0.5 * shape_par * suction)
    conduct = sat_cond * jnp.exp(shape_par * suction) * active.astype(jnp.float32)
    moisture = porous * (0.15 + 0.85 * wetness)
    below = shifted(jnp.concatenate([pressure[:1], conduct[:1]], axis=0), "depth", -1)
    inner = face_flux(pressure[:-1], conduct[:-1], pressure[1:], conduct[1:])
    last_face = face_flux(pressure[-1], conduct[-1], below[0], below[1])
    above = shifted(last_face, "depth", 1)
    upper = jnp.concatenate([jnp.where(is_top, rain, above)[None], inner], axis=0)
    lower_last = last_face
    trans_part = jnp.sum(conduct, axis=0)
    store_part = jnp.sum(0.85 * porous * (1.0 - wetness), axis=0)
    charge_part = jnp.sum(conduct * wetness, axis=0)
    tile_cols = head_old.shape[1]
    summed = lax.psum((trans_part, store_part, charge_part), "depth")
    trans_sum = lax.dynamic_slice_in_dim(summed[0], depth_index * tile_cols, tile_cols, 1)
    store_sum = lax.dynamic_slice_in_dim(summed[1], depth_index * tile_cols, tile_cols, 1)
    charge_sum = lax.dynamic_slice_in_dim(summed[2], depth_index * tile_cols, tile_cols, 1)
    trans = trans_sum * layer_thick
    store = spec_yield + store_sum * layer_thick
    recharge = leak_rate * (charge_sum * layer_thick)
    river = jnp.where(
        cell_code == 1,
        jnp.float32(river_cond),
        jnp.where(cell_code == 2, jnp.float32(fixed_cond), jnp.float32(0.0)),
    )
    base = store + river
    rhs = store * head_old + recharge + river * section
    trans_pad = with_halo(trans, (("strips", 0), ("depth", 1)), 1)
    head = head_old
    for sweep_id in range(SWEEPS):
        head_pad = with_halo(head, (("strips", 0), ("depth", 1)), 1)
        head = sweep(head_pad, trans_pad, base, rhs)
    full_head = lax.all_gather(head, "depth", axis=1, tiled=True)
    bottom = conduct[-1] * ((pressure[-1] - full_head) / (0.5 * layer_thick) + 1.0)
    lower_last = jnp.where(is_bottom, bottom, lower_last)
    lower = jnp.concatenate([inner, lower_last[None]], axis=0)
    moisture_new = moisture + soil_step / layer_thick * (upper - lower)
    return (moisture_new, head)


def solution(mesh):
    in_specs = (
        P("depth", "strips", None),
        P("depth", "strips", None),
        P("depth", "strips", None),
        P("strips", None),
        P(),
        P(),
        P(),
        P("strips", "depth"),
        P("strips", "depth"),
        P("strips", "depth"),
    )
    out_specs = (P("depth", "strips", None), P("strips", "depth"))
    return jax.shard_map(shards, mesh=mesh, in_specs=in_specs, out_specs=out_specs, check_vma=False)
```

profile of v0, /device:TPU:104, one launch (start us, length us, event | category | flops | bytes accessed | tf_op | source)
XLA Modules:
  0.0 211.3 jit_solution(2209304728471105237)
XLA Ops:
  7.2 0.0 all-reduce.3.cloned.1.call-start
  7.3 9.7 %broadcast_compare_fusion.11 = (pred[8,128,1024]{2,1,0:T(8,128)(4,1)S(1)}, pred[8,128,1024]{2,1,0:T(8,128)(4,1)S(1)}, pred[8,128,1024]{2,1,0:T(8,128)(4,1)S(1)},...) fusion(s32[8,128,1024]{2,1,0:T(8,128)} %param.11), kind=kLoop, calls=%fused_computation.23 | loop fusion | flops 12582912 | bytes 16777216 | tf_op jit(solution)/shard_map/eq | solution.py:43
  17.0 0.7 fusion.65
  17.7 0.7 fusion.64
  18.4 0.7 fusion.63
  19.1 40.2 %fusion.53 = (f32[128,1024]{1,0:T(8,128)}, f32[128,1024]{1,0:T(8,128)}, f32[128,1024]{1,0:T(8,128)}, f32[8,128,1024]{2,1,0:T(8,128)}, f32[8,128,1024]{2,1,0:T(8,128)}, /*index=5*/f32[8,128,1024]{2,1,0:T(8,128)}) fusion(pred[8,128,1024]{2,1,0:T(8,128)(4,1)S(1)} %get-tuple-element.27, f32[]{:T(128)} %bitcast.11, ...), kind=kLoop, calls=%fused_computation.123 | loop fusion | flops 86638592 | bytes 35127440 | tf_op jit(solution)/shard_map/reduce_sum | solution.py:86
  59.3 0.0 all-reduce.3.cloned.1.call-update
  59.4 6.4 %collective-permute-start.6 = (f32[1,256]{1,0:T(1,128)S(1)}, f32[1,256]{1,0:T(1,128)S(1)}, u32[]{:S(2)}, u32[]{:S(2)}) collective-permute-start(f32[1,256]{1,0:T(1,128)S(1)} %get-tuple-element.44), channel_id=1, source_target_pairs={{1,0},{2,1},{3,2},{4,3},{5,4},{6,5},{7,6},{8,7},{9,8},{10,9},{11,1... | collective-permute-start | bytes 3080 | tf_op jit(solution)/shard_map/ppermute | solution.py:33
  65.7 1.9 collective-permute-start.7
  67.7 8.0 %collective-permute-done.7 = f32[1,256]{1,0:T(1,128)S(1)} collective-permute-done((f32[1,256]{1,0:T(1,128)S(1)}, f32[1,256]{1,0:T(1,128)S(1)}, u32[]{:S(2)}, u32[]{:S(2)}) %collective-permute-start.7) | collective-permute-done | bytes 1056 | tf_op jit(solution)/shard_map/ppermute | solution.py:31
  75.7 32.8 %all-reduce.3.cloned.1.call-done = (f32[128,1024]{1,0:T(8,128)}, f32[128,1024]{1,0:T(8,128)}, f32[128,1024]{1,0:T(8,128)}) async-done(((f32[128,1024]{1,0:T(8,128)}, f32[128,1024]{1,0:T(8,128)}, f32[128,1024]{1,0:T(8,128)}), (f32[128,1024]{1,0:T(8,128)}, f32[128,1024]{1,0:T(8,128)}, f32[128,1024]{1,0:T(8,128)})) %all-reduce.3.cloned.1.call-update) | async-done | bytes 1572880 | tf_op jit(solution)/shard_map/psum | solution.py:90
  108.5 0.9 dynamic-slice_multiply_fusion
  109.4 6.6 %collective-permute-start.2 = (f32[1,256]{1,0:T(1,128)S(1)}, f32[1,256]{1,0:T(1,128)S(1)}, u32[]{:S(2)}, u32[]{:S(2)}) collective-permute-start(f32[1,256]{1,0:T(1,128)S(1)} %get-tuple-element.42), channel_id=1, source_target_pairs={{1,0},{2,1},{3,2},{4,3},{5,4},{6,5},{7,6},{8,7},{9,8},{10,9},{11,1... | collective-permute-start | bytes 3080 | tf_op jit(solution)/shard_map/ppermute | solution.py:33
  116.1 1.9 collective-permute-start.3
  118.0 0.1 fusion.58
  118.1 3.2 %collective-permute-start.8 = (f32[130,1]{1,0:T(8,128)S(1)}, f32[130,1]{1,0:T(8,128)S(1)}, u32[]{:S(2)}, u32[]{:S(2)}) collective-permute-start(f32[130,1]{1,0:T(8,128)S(1)} %get-tuple-element.35), channel_id=1, source_target_pairs={{32,0},{64,32},{96,64},{33,1},{65,33},{97,65},{34,2},{66,34},{98,6... | collective-permute-start | bytes 1568 | tf_op jit(solution)/shard_map/ppermute | solution.py:33
  121.4 1.9 collective-permute-start.9
  123.3 2.8 %collective-permute-done.3 = f32[1,256]{1,0:T(1,128)S(1)} collective-permute-done((f32[1,256]{1,0:T(1,128)S(1)}, f32[1,256]{1,0:T(1,128)S(1)}, u32[]{:S(2)}, u32[]{:S(2)}) %collective-permute-start.3) | collective-permute-done | bytes 1056 | tf_op jit(solution)/shard_map/ppermute | solution.py:31
  126.1 0.1 fusion.57
  126.2 2.1 collective-permute-start.4
  128.3 2.2 %collective-permute-start.5 = (f32[130,1]{1,0:T(8,128)S(1)}, f32[130,1]{1,0:T(8,128)S(1)}, u32[]{:S(2)}, u32[]{:S(2)}) collective-permute-start(f32[130,1]{1,0:T(8,128)S(1)} %get-tuple-element.33), channel_id=1, source_target_pairs={{0,32},{32,64},{64,96},{1,33},{33,65},{65,97},{2,34},{34,66},{66,9... | collective-permute-start | bytes 1568 | tf_op jit(solution)/shard_map/ppermute | solution.py:31
  130.6 3.3 %collective-permute-done.5 = f32[130,1]{1,0:T(8,128)S(1)} collective-permute-done((f32[130,1]{1,0:T(8,128)S(1)}, f32[130,1]{1,0:T(8,128)S(1)}, u32[]{:S(2)}, u32[]{:S(2)}) %collective-permute-start.5) | collective-permute-done | bytes 552 | tf_op jit(solution)/shard_map/ppermute | solution.py:31
  133.9 1.4 fusion.38
  135.3 6.3 %collective-permute-start.10 = (f32[1,256]{1,0:T(1,128)S(1)}, f32[1,256]{1,0:T(1,128)S(1)}, u32[]{:S(2)}, u32[]{:S(2)}) collective-permute-start(f32[1,256]{1,0:T(1,128)S(1)} %get-tuple-element.40), channel_id=1, source_target_pairs={{1,0},{2,1},{3,2},{4,3},{5,4},{6,5},{7,6},{8,7},{9,8},{10,9},{11,1... | collective-permute-start | bytes 3080 | tf_op jit(solution)/shard_map/ppermute | solution.py:33
  141.6 1.9 collective-permute-start.11
  143.6 1.1 slice.339
  144.7 7.0 %collective-permute-done.11 = f32[1,256]{1,0:T(1,128)S(1)} collective-permute-done((f32[1,256]{1,0:T(1,128)S(1)}, f32[1,256]{1,0:T(1,128)S(1)}, u32[]{:S(2)}, u32[]{:S(2)}) %collective-permute-start.11) | collective-permute-done | bytes 1056 | tf_op jit(solution)/shard_map/ppermute | solution.py:31
  151.6 0.1 fusion.56
  151.7 1.9 collective-permute-start.12
  153.6 2.4 %collective-permute-start.13 = (f32[130,1]{1,0:T(8,128)S(1)}, f32[130,1]{1,0:T(8,128)S(1)}, u32[]{:S(2)}, u32[]{:S(2)}) collective-permute-start(f32[130,1]{1,0:T(8,128)S(1)} %get-tuple-element.32), channel_id=1, source_target_pairs={{0,32},{32,64},{64,96},{1,33},{33,65},{65,97},{2,34},{34,66},{66,9... | collective-permute-start | bytes 1568 | tf_op jit(solution)/shard_map/ppermute | solution.py:31
  156.1 0.1 pad_maximum_fusion
  156.2 3.2 %collective-permute-start = (f32[2,128,1024]{2,1,0:T(8,128)S(1)}, f32[2,128,1024]{2,1,0:T(8,128)S(1)}, u32[]{:S(2)}, u32[]{:S(2)}) collective-permute-start(f32[2,128,1024]{2,1,0:T(8,128)S(1)} %pad_maximum_fusion), channel_id=1, source_target_pairs={{32,0},{64,32},{96,64},{33,1},{65,33},{97,65},{34,2},{66,34},{98,6... | collective-permute-start | bytes 3145736 | tf_op jit(solution)/shard_map/ppermute | solution.py:20
  159.3 1.3 fusion.28
  160.6 1.9 collective-permute-start.14
  162.6 3.9 %collective-permute-start.15 = (f32[1,256]{1,0:T(1,128)S(1)}, f32[1,256]{1,0:T(1,128)S(1)}, u32[]{:S(2)}, u32[]{:S(2)}) collective-permute-start(f32[1,256]{1,0:T(1,128)S(1)} %get-tuple-element.37), channel_id=1, source_target_pairs={{0,1},{1,2},{2,3},{3,4},{4,5},{5,6},{6,7},{7,8},{8,9},{9,10},{10,1... | collective-permute-start | bytes 3080 | tf_op jit(solution)/shard_map/ppermute | solution.py:31
  166.5 6.0 %collective-permute-done.15 = f32[1,256]{1,0:T(1,128)S(1)} collective-permute-done((f32[1,256]{1,0:T(1,128)S(1)}, f32[1,256]{1,0:T(1,128)S(1)}, u32[]{:S(2)}, u32[]{:S(2)}) %collective-permute-start.15) | collective-permute-done | bytes 1056 | tf_op jit(solution)/shard_map/ppermute | solution.py:31
  172.6 0.1 fusion.55
  172.6 1.9 collective-permute-start.16
  174.6 2.4 %collective-permute-start.17 = (f32[130,1]{1,0:T(8,128)S(1)}, f32[130,1]{1,0:T(8,128)S(1)}, u32[]{:S(2)}, u32[]{:S(2)}) collective-permute-start(f32[130,1]{1,0:T(8,128)S(1)} %get-tuple-element.30), channel_id=1, source_target_pairs={{0,32},{32,64},{64,96},{1,33},{33,65},{65,97},{2,34},{34,66},{66,9... | collective-permute-start | bytes 1568 | tf_op jit(solution)/shard_map/ppermute | solution.py:31
  177.0 3.2 %collective-permute-done.17 = f32[130,1]{1,0:T(8,128)S(1)} collective-permute-done((f32[130,1]{1,0:T(8,128)S(1)}, f32[130,1]{1,0:T(8,128)S(1)}, u32[]{:S(2)}, u32[]{:S(2)}) %collective-permute-start.17) | collective-permute-done | bytes 552 | tf_op jit(solution)/shard_map/ppermute | solution.py:31
  180.2 1.3 fusion.18
  181.5 6.5 %all_gather.3 = f32[128,1024]{1,0:T(8,128)S(1)} all-gather(f32[128,256]{1,0:T(8,128)S(1)} %fusion.18), channel_id=1, replica_groups=mesh['depth'=4,'strips'=32] {'depth'}, dimensions={1}, use_global_device_ids=true | all-gather | bytes 655360 | tf_op jit(solution)/shard_map/all_gather | solution.py:109
  188.0 2.3 %fusion.14 = (f32[1,128,1024]{2,1,0:T(8,128)S(1)}, f32[128,1024]{1,0:T(8,128)}) fusion(f32[128,1024]{1,0:T(8,128)S(1)} %all_gather.3, f32[8,128,1024]{2,1,0:T(8,128)} %get-tuple-element.16, f32[8,128,1024]{2,1,0:T(8,128)} %param.10, pred[]{:T(512)S(6)} %eq.91, f32[2,128,1024]{2,1,0:T(8,128)S(1)} %collective-permute-done), kind=kLoop, calls=%fused_computation.39 | loop fusion | flops 1441792 | bytes 3670017 | tf_op jit(solution)/shard_map/broadcast_in_dim | solution.py:112
  190.3 2.2 %collective-permute-start.1 = (f32[128,1024]{1,0:T(8,128)}, f32[128,1024]{1,0:T(8,128)S(1)}, u32[]{:S(2)}, u32[]{:S(2)}) collective-permute-start(f32[128,1024]{1,0:T(8,128)} %get-tuple-element.9), channel_id=1, source_target_pairs={{0,32},{32,64},{64,96},{1,33},{33,65},{65,97},{2,34},{34,66},{66,9... | collective-permute-start | bytes 1572872 | tf_op jit(solution)/shard_map/ppermute | solution.py:20
  192.6 7.3 %fusion.3 = f32[7,128,1024]{2,1,0:T(8,128)S(1)} fusion(f32[8,128,1024]{2,1,0:T(8,128)} %get-tuple-element.16, f32[8,128,1024]{2,1,0:T(8,128)} %param.10), kind=kLoop, calls=%fused_computation.11 | loop fusion | flops 5505024 | bytes 18350080 | tf_op jit(solution)/shard_map/mul | solution.py:48
  199.9 1.1 collective-permute-done.1
  201.0 0.1 select_bitcast_fusion
  201.1 3.4 %fusion.1 = f32[8,128,1024]{2,1,0:T(8,128)} fusion(f32[7,128,1024]{2,1,0:T(8,128)S(1)} %fusion.3, f32[1,128,1024]{2,1,0:T(8,128)S(1)} %select_bitcast_fusion, f32[1,128,1024]{2,1,0:T(8,128)S(1)} %get-tuple-element.8, f32[8,128,1024]{2,1,0:T(8,128)S(1)} %copy-done.1, f32[8,128,1024]{2,1,0:T(8,128)S(1)} %copy-done.2), kind=kLoop, calls=%fused_computation.2 | loop fusion | flops 8388608 | bytes 17301504 | tf_op jit(solution)/shard_map/add | solution.py:113
  (45 shorter events, 0.2 us)
Async XLA Ops:
  7.2 9.8 %copy-start.9 = (f32[12]{0:T(128)S(1)}, f32[12]{0:T(128)}, u32[]{:S(2)}) copy-start(f32[12]{0:T(128)} %param.16) | copy-start | bytes 148
  7.2 10.5 %copy-start.10 = (f32[12]{0:T(128)S(1)}, f32[12]{0:T(128)}, u32[]{:S(2)}) copy-start(f32[12]{0:T(128)} %param.15) | copy-start | bytes 148
  7.2 11.2 %copy-start.11 = (f32[12]{0:T(128)S(1)}, f32[12]{0:T(128)}, u32[]{:S(2)}) copy-start(f32[12]{0:T(128)} %param.14) | copy-start | bytes 148
  7.2 101.3 %all-reduce.3.cloned.1.call-start = ((), (), s32[]{:S(2)}) async-start(), calls=%async_computation | async-start | bytes 3145728 | tf_op jit(solution)/shard_map/psum | solution.py:90
  7.2 11.8 %copy-start = (f32[8,128,1024]{2,1,0:T(8,128)S(1)}, f32[8,128,1024]{2,1,0:T(8,128)}, u32[]{:S(2)}) copy-start(f32[8,128,1024]{2,1,0:T(8,128)} %param.10) | copy-start | bytes 12582916
  7.3 11.8 %copy-start.3 = (s32[8,128,1024]{2,1,0:T(8,128)S(1)}, s32[8,128,1024]{2,1,0:T(8,128)}, u32[]{:S(2)}) copy-start(s32[8,128,1024]{2,1,0:T(8,128)} %param.12) | copy-start | bytes 12582916
  19.1 40.2 %copy-start.4 = (f32[128,256]{1,0:T(8,128)S(1)}, f32[128,256]{1,0:T(8,128)}, u32[]{:S(2)}) copy-start(f32[128,256]{1,0:T(8,128)} %param.17) | copy-start | bytes 393220
  19.1 114.8 %copy-start.7 = (f32[128,256]{1,0:T(8,128)S(1)}, f32[128,256]{1,0:T(8,128)}, u32[]{:S(2)}) copy-start(f32[128,256]{1,0:T(8,128)} %param.19) | copy-start | bytes 393220
  19.1 114.8 %copy-start.8 = (s32[128,256]{1,0:T(8,128)S(1)}, s32[128,256]{1,0:T(8,128)}, u32[]{:S(2)}) copy-start(s32[128,256]{1,0:T(8,128)} %param.18) | copy-start | bytes 393220
  59.3 96.7 %slice-start = ((f32[8,128,1024]{2,1,0:T(8,128)}), f32[1,128,1024]{2,1,0:T(8,128)S(1)}, s32[]{:S(2)}) async-start(f32[8,128,1024]{2,1,0:T(8,128)} %param.10), calls=%async_computation.1 | async-start | bytes 1048576 | tf_op jit(solution)/shard_map/slice | solution.py:80
  59.4 8.3 %collective-permute-start.6 = (f32[1,256]{1,0:T(1,128)S(1)}, f32[1,256]{1,0:T(1,128)S(1)}, u32[]{:S(2)}, u32[]{:S(2)}) collective-permute-start(f32[1,256]{1,0:T(1,128)S(1)} %get-tuple-element.44), channel_id=1, source_target_pairs={{1,0},{2,1},{3,2},{4,3},{5,4},{6,5},{7,6},{8,7},{9,8},{10,9},{11,1... | collective-permute-start | bytes 3080 | tf_op jit(solution)/shard_map/ppermute | solution.py:33
  65.7 10.0 %collective-permute-start.7 = (f32[1,256]{1,0:T(1,128)S(1)}, f32[1,256]{1,0:T(1,128)S(1)}, u32[]{:S(2)}, u32[]{:S(2)}) collective-permute-start(f32[1,256]{1,0:T(1,128)S(1)} %get-tuple-element.43), channel_id=1, source_target_pairs={{0,1},{1,2},{2,3},{3,4},{4,5},{5,6},{6,7},{7,8},{8,9},{9,10},{10,1... | collective-permute-start | bytes 3080 | tf_op jit(solution)/shard_map/ppermute | solution.py:31
  109.4 13.8 %collective-permute-start.2 = (f32[1,256]{1,0:T(1,128)S(1)}, f32[1,256]{1,0:T(1,128)S(1)}, u32[]{:S(2)}, u32[]{:S(2)}) collective-permute-start(f32[1,256]{1,0:T(1,128)S(1)} %get-tuple-element.42), channel_id=1, source_target_pairs={{1,0},{2,1},{3,2},{4,3},{5,4},{6,5},{7,6},{8,7},{9,8},{10,9},{11,1... | collective-permute-start | bytes 3080 | tf_op jit(solution)/shard_map/ppermute | solution.py:33
  116.1 10.0 %collective-permute-start.3 = (f32[1,256]{1,0:T(1,128)S(1)}, f32[1,256]{1,0:T(1,128)S(1)}, u32[]{:S(2)}, u32[]{:S(2)}) collective-permute-start(f32[1,256]{1,0:T(1,128)S(1)} %get-tuple-element.41), channel_id=1, source_target_pairs={{0,1},{1,2},{2,3},{3,4},{4,5},{5,6},{6,7},{7,8},{8,9},{9,10},{10,1... | collective-permute-start | bytes 3080 | tf_op jit(solution)/shard_map/ppermute | solution.py:31
  118.1 12.4 %collective-permute-start.8 = (f32[130,1]{1,0:T(8,128)S(1)}, f32[130,1]{1,0:T(8,128)S(1)}, u32[]{:S(2)}, u32[]{:S(2)}) collective-permute-start(f32[130,1]{1,0:T(8,128)S(1)} %get-tuple-element.35), channel_id=1, source_target_pairs={{32,0},{64,32},{96,64},{33,1},{65,33},{97,65},{34,2},{66,34},{98,6... | collective-permute-start | bytes 1568 | tf_op jit(solution)/shard_map/ppermute | solution.py:33
  121.4 9.2 %collective-permute-start.9 = (f32[130,1]{1,0:T(8,128)S(1)}, f32[130,1]{1,0:T(8,128)S(1)}, u32[]{:S(2)}, u32[]{:S(2)}) collective-permute-start(f32[130,1]{1,0:T(8,128)S(1)} %get-tuple-element.36), channel_id=1, source_target_pairs={{0,32},{32,64},{64,96},{1,33},{33,65},{65,97},{2,34},{34,66},{66,9... | collective-permute-start | bytes 1568 | tf_op jit(solution)/shard_map/ppermute | solution.py:31
  126.2 4.4 %collective-permute-start.4 = (f32[130,1]{1,0:T(8,128)S(1)}, f32[130,1]{1,0:T(8,128)S(1)}, u32[]{:S(2)}, u32[]{:S(2)}) collective-permute-start(f32[130,1]{1,0:T(8,128)S(1)} %get-tuple-element.34), channel_id=1, source_target_pairs={{32,0},{64,32},{96,64},{33,1},{65,33},{97,65},{34,2},{66,34},{98,6... | collective-permute-start | bytes 1568 | tf_op jit(solution)/shard_map/ppermute | solution.py:33
  128.3 5.6 %collective-permute-start.5 = (f32[130,1]{1,0:T(8,128)S(1)}, f32[130,1]{1,0:T(8,128)S(1)}, u32[]{:S(2)}, u32[]{:S(2)}) collective-permute-start(f32[130,1]{1,0:T(8,128)S(1)} %get-tuple-element.33), channel_id=1, source_target_pairs={{0,32},{32,64},{64,96},{1,33},{33,65},{65,97},{2,34},{34,66},{66,9... | collective-permute-start | bytes 1568 | tf_op jit(solution)/shard_map/ppermute | solution.py:31
  135.3 9.4 %collective-permute-start.10 = (f32[1,256]{1,0:T(1,128)S(1)}, f32[1,256]{1,0:T(1,128)S(1)}, u32[]{:S(2)}, u32[]{:S(2)}) collective-permute-start(f32[1,256]{1,0:T(1,128)S(1)} %get-tuple-element.40), channel_id=1, source_target_pairs={{1,0},{2,1},{3,2},{4,3},{5,4},{6,5},{7,6},{8,7},{9,8},{10,9},{11,1... | collective-permute-start | bytes 3080 | tf_op jit(solution)/shard_map/ppermute | solution.py:33
  141.6 10.0 %collective-permute-start.11 = (f32[1,256]{1,0:T(1,128)S(1)}, f32[1,256]{1,0:T(1,128)S(1)}, u32[]{:S(2)}, u32[]{:S(2)}) collective-permute-start(f32[1,256]{1,0:T(1,128)S(1)} %get-tuple-element.39), channel_id=1, source_target_pairs={{0,1},{1,2},{2,3},{3,4},{4,5},{5,6},{6,7},{7,8},{8,9},{9,10},{10,1... | collective-permute-start | bytes 3080 | tf_op jit(solution)/shard_map/ppermute | solution.py:31
  151.7 7.6 %collective-permute-start.12 = (f32[130,1]{1,0:T(8,128)S(1)}, f32[130,1]{1,0:T(8,128)S(1)}, u32[]{:S(2)}, u32[]{:S(2)}) collective-permute-start(f32[130,1]{1,0:T(8,128)S(1)} %get-tuple-element.31), channel_id=1, source_target_pairs={{32,0},{64,32},{96,64},{33,1},{65,33},{97,65},{34,2},{66,34},{98,6... | collective-permute-start | bytes 1568 | tf_op jit(solution)/shard_map/ppermute | solution.py:33
  153.6 5.7 %collective-permute-start.13 = (f32[130,1]{1,0:T(8,128)S(1)}, f32[130,1]{1,0:T(8,128)S(1)}, u32[]{:S(2)}, u32[]{:S(2)}) collective-permute-start(f32[130,1]{1,0:T(8,128)S(1)} %get-tuple-element.32), channel_id=1, source_target_pairs={{0,32},{32,64},{64,96},{1,33},{33,65},{65,97},{2,34},{34,66},{66,9... | collective-permute-start | bytes 1568 | tf_op jit(solution)/shard_map/ppermute | solution.py:31
  156.2 31.8 %collective-permute-start = (f32[2,128,1024]{2,1,0:T(8,128)S(1)}, f32[2,128,1024]{2,1,0:T(8,128)S(1)}, u32[]{:S(2)}, u32[]{:S(2)}) collective-permute-start(f32[2,128,1024]{2,1,0:T(8,128)S(1)} %pad_maximum_fusion), channel_id=1, source_target_pairs={{32,0},{64,32},{96,64},{33,1},{65,33},{97,65},{34,2},{66,34},{98,6... | collective-permute-start | bytes 3145736 | tf_op jit(solution)/shard_map/ppermute | solution.py:20
  160.6 5.9 %collective-permute-start.14 = (f32[1,256]{1,0:T(1,128)S(1)}, f32[1,256]{1,0:T(1,128)S(1)}, u32[]{:S(2)}, u32[]{:S(2)}) collective-permute-start(f32[1,256]{1,0:T(1,128)S(1)} %get-tuple-element.38), channel_id=1, source_target_pairs={{1,0},{2,1},{3,2},{4,3},{5,4},{6,5},{7,6},{8,7},{9,8},{10,9},{11,1... | collective-permute-start | bytes 3080 | tf_op jit(solution)/shard_map/ppermute | solution.py:33
  162.6 10.0 %collective-permute-start.15 = (f32[1,256]{1,0:T(1,128)S(1)}, f32[1,256]{1,0:T(1,128)S(1)}, u32[]{:S(2)}, u32[]{:S(2)}) collective-permute-start(f32[1,256]{1,0:T(1,128)S(1)} %get-tuple-element.37), channel_id=1, source_target_pairs={{0,1},{1,2},{2,3},{3,4},{4,5},{5,6},{6,7},{7,8},{8,9},{9,10},{10,1... | collective-permute-start | bytes 3080 | tf_op jit(solution)/shard_map/ppermute | solution.py:31
  172.6 4.3 %collective-permute-start.16 = (f32[130,1]{1,0:T(8,128)S(1)}, f32[130,1]{1,0:T(8,128)S(1)}, u32[]{:S(2)}, u32[]{:S(2)}) collective-permute-start(f32[130,1]{1,0:T(8,128)S(1)} %get-tuple-element.29), channel_id=1, source_target_pairs={{32,0},{64,32},{96,64},{33,1},{65,33},{97,65},{34,2},{66,34},{98,6... | collective-permute-start | bytes 1568 | tf_op jit(solution)/shard_map/ppermute | solution.py:33
  174.6 5.6 %collective-permute-start.17 = (f32[130,1]{1,0:T(8,128)S(1)}, f32[130,1]{1,0:T(8,128)S(1)}, u32[]{:S(2)}, u32[]{:S(2)}) collective-permute-start(f32[130,1]{1,0:T(8,128)S(1)} %get-tuple-element.30), channel_id=1, source_target_pairs={{0,32},{32,64},{64,96},{1,33},{33,65},{65,97},{2,34},{34,66},{66,9... | collective-permute-start | bytes 1568 | tf_op jit(solution)/shard_map/ppermute | solution.py:31
  181.5 18.4 %copy-start.5 = (f32[128,256]{1,0:T(8,128)}, f32[128,256]{1,0:T(8,128)S(1)}, u32[]{:S(2)}) copy-start(f32[128,256]{1,0:T(8,128)S(1)} %fusion.18) | copy-start | bytes 393220
  190.3 10.7 %collective-permute-start.1 = (f32[128,1024]{1,0:T(8,128)}, f32[128,1024]{1,0:T(8,128)S(1)}, u32[]{:S(2)}, u32[]{:S(2)}) collective-permute-start(f32[128,1024]{1,0:T(8,128)} %get-tuple-element.9), channel_id=1, source_target_pairs={{0,32},{32,64},{64,96},{1,33},{33,65},{65,97},{2,34},{34,66},{66,9... | collective-permute-start | bytes 1572872 | tf_op jit(solution)/shard_map/ppermute | solution.py:20
  192.6 8.4 %copy-start.6 = (f32[128,1024]{1,0:T(8,128)S(1)}, f32[128,1024]{1,0:T(8,128)}, u32[]{:S(2)}) copy-start(f32[128,1024]{1,0:T(8,128)} %param.13) | copy-start | bytes 1572868
  192.6 8.5 %copy-start.1 = (f32[8,128,1024]{2,1,0:T(8,128)S(1)}, f32[8,128,1024]{2,1,0:T(8,128)}, u32[]{:S(2)}) copy-start(f32[8,128,1024]{2,1,0:T(8,128)} %get-tuple-element.14) | copy-start | bytes 12582916
  192.6 8.5 %copy-start.2 = (f32[8,128,1024]{2,1,0:T(8,128)S(1)}, f32[8,128,1024]{2,1,0:T(8,128)}, u32[]{:S(2)}) copy-start(f32[8,128,1024]{2,1,0:T(8,128)} %get-tuple-element.15) | copy-start | bytes 12582916
Sparse Core Ops, SparseCore 0:
  59.5 49.0 all-reduce.2
where the time goes:
time: 214 us; the launch traced here: 211 us
  other arithmetic  67.9 us (32%)
  waiting for transfers between devices  64.3 us (30%)
  starting transfers between devices  54.5 us (25%)
  between operations  14.5 us (7%)
  blocking collectives  6.5 us (3%)
  local copies, waits for them, and re-layouts  3.56 us (2%)
    reduce_sum x1, other arithmetic, shards(): trans_part = jnp.sum(conduct, axis=0)  40.2 us
    psum x1, waiting for transfers between devices, shards(): summed = lax.psum((trans_part, store_part, charge_part), 'depth')  32.8 us
    ppermute x8, starting transfers between devices, with_halo(): lax.ppermute(head, axis, [((i + 1) % count, i) for i in range(ends)])  30.4 us
    ppermute x8, waiting for transfers between devices, with_halo(): lax.ppermute(tail, axis, [(i, (i + 1) % count) for i in range(ends)])  30.4 us
    ppermute x8, starting transfers between devices, with_halo(): lax.ppermute(tail, axis, [(i, (i + 1) % count) for i in range(ends)])  18.7 us
    eq x1, other arithmetic, lookup(): texture == class_id  9.72 us
    mul x1, other arithmetic, face_flux(): return 0.5 * (cond_up + cond_low) * ((psi_up - psi_low) / layer_thick + 1.0)  7.25 us
    all_gather x1, blocking collectives, shards(): full_head = lax.all_gather(head, 'depth', axis=1, tiled=True)  6.5 us
  transfers between devices with their start and end apart: 19, of which 8 were waited for; matrix products, arithmetic and copies ran while one was open for 5% of the time, Pallas kernels for 0%

commit v1 on v0

v1 whole, which is shorter than its diff:
```python
import functools
import math

import jax
import jax.numpy as jnp
from jax import lax
from jax.experimental import pallas as pl
from jax.experimental.pallas import tpu as pltpu
from jax.sharding import PartitionSpec as P

MESH = pl.DeviceIdType.MESH
SWEEPS = 3

layer_thick = 0.05
soil_step = 0.0002
spec_yield = 0.02
leak_rate = 0.5
river_cond = 0.5
fixed_cond = 3.0
face_scale = soil_step / layer_thick

R = 16
RE = 32
PAD = 16
LANES = 128


def pick(table, index):
    dims = lax.GatherDimensionNumbers(
        offset_dims=(),
        collapsed_slice_dims=(0,),
        start_index_map=(0,),
        operand_batching_dims=(1,),
        start_indices_batching_dims=(1,),
    )
    rows = [
        lax.gather(
            table,
            index[8 * i : 8 * i + 8, :, None],
            dims,
            slice_sizes=(1, 1),
            mode=lax.GatherScatterMode.PROMISE_IN_BOUNDS,
        )
        for i in range(index.shape[0] // 8)
    ]
    return jnp.concatenate(rows, axis=0)


def flux(psi_up, cond_up, psi_low, cond_low):
    return (cond_up + cond_low) * (
        (psi_up - psi_low) * (0.5 * face_scale / layer_thick) + 0.5 * face_scale
    )


def kernel(
    strips, ks, al, th, p_hbm, t_hbm, a_hbm, rain_hbm, h_hbm, code_hbm, sec_hbm,
    moist, head,
    pbuf, tbuf, abuf, rain, h0, code, sec, tabs, part, recv1, xs, recv2, c0, c7,
    dn_p, dn_c, up_p, up_c, fb_out, fb_in, fa_out, fa_in,
    E, H, C, colsend, colrecv, heads,
    load_sem, misc_sem, s1_send, s1_recv, s2_send, s2_recv,
    face_send, face_recv, col_send, col_recv, row_send, row_recv, head_send, head_recv,
):
    layers, rows_all, cols_all = pbuf.shape
    chunks, edges = rows_all // R, rows_all // RE
    tile = h0.shape[1]
    wide = tile + 2 * LANES
    cols_a = dn_p.shape[1]
    part_a, part_b = pl.ds(0, cols_a), pl.ds(cols_a, cols_all - cols_a)
    body = pl.ds(PAD, rows_all)
    mid = pl.ds(LANES, tile)
    last = layers - 1
    depth, strip = lax.axis_index("depth"), lax.axis_index("strips")
    core, chip = depth % 2, depth // 2
    mate = {"depth": chip * 2 + 1 - core}
    cross = {"depth": (depth + 2) % 4}
    above, below = {"depth": depth - 1}, {"depth": depth + 1}
    north, south = {"strips": strip - 1}, {"strips": strip + 1}
    has_up, has_down = depth > 0, depth < 3
    has_north, has_south = strip > 0, strip < strips - 1

    def remote(src, dst, send, recv, device):
        return pltpu.make_async_remote_copy(
            src_ref=src, dst_ref=dst, send_sem=send, recv_sem=recv,
            device_id=device, device_id_type=MESH,
        )

    barrier = pltpu.get_barrier_semaphore()

    def greet(device):
        pl.semaphore_signal(barrier, inc=1, device_id=device, device_id_type=MESH)

    for step in (1, 2, 3):
        greet({"depth": (depth + step) % 4})
    pl.when(has_north)(lambda: greet(north))
    pl.when(has_south)(lambda: greet(south))

    def load(which, chunk):
        src, dst = ((p_hbm, pbuf), (t_hbm, tbuf), (a_hbm, abuf))[which]
        where = pl.ds(pl.multiple_of(chunk * R, R), R)
        return pltpu.make_async_copy(src.at[:, where, :], dst.at[:, where, :], load_sem.at[which, chunk])

    small = [
        pltpu.make_async_copy(src, dst, misc_sem.at[i])
        for i, (src, dst) in enumerate(((h_hbm, h0), (code_hbm, code), (sec_hbm, sec), (rain_hbm, rain)))
    ]
    for i in range(chunks):
        for which in range(3):
            load(which, (i + chunks - 1) % chunks).start()
    for copy in small:
        copy.start()

    scales = (1.0, 0.5 * math.log2(math.e), 0.85)
    row = lax.broadcasted_iota(jnp.int32, (8, LANES), 0)
    for i, (ref, scale) in enumerate(zip((ks, al, th), scales)):
        low = high = jnp.zeros((8, LANES), jnp.float32)
        for c in range(ref.shape[0]):
            value = ref[c] * scale
            if c < 8:
                low = jnp.where(row == c, value, low)
            else:
                high = jnp.where(row == c - 8, value, high)
        tabs[i, 0] = low
        tabs[i, 1] = high

    def blank(first, count):
        for q in range(4):
            E[q, first : first + count, :] = jnp.full((count, wide), 1.0 if q == 1 else 0.0, jnp.float32)

    blank(0, 8)
    blank(PAD + rows_all + 8, 8)
    pl.when(strip == 0)(lambda: blank(8, 8))
    pl.when(strip == strips - 1)(lambda: blank(PAD + rows_all, 8))
    for side in range(2):
        H[side, 0:8, :] = jnp.zeros((8, wide), jnp.float32)
        H[side, 2 * PAD + rows_all - 8 :, :] = jnp.zeros((8, wide), jnp.float32)

    def stage1(chunk):
        return remote(
            part.at[chunk, 1 - core], recv1.at[chunk], s1_send.at[chunk], s1_recv.at[chunk], mate
        )

    def stage2(chunk):
        return remote(xs.at[chunk], recv2.at[chunk], s2_send.at[chunk], s2_recv.at[chunk], cross)

    def column_pass(chunk):
        for which in range(3):
            load(which, chunk).wait()
        where = pl.ds(pl.multiple_of(chunk * R, R), R)

        def lane_tile(block, half):
            cols = pl.ds(pl.multiple_of(block * tile + half * LANES, LANES), LANES)
            total = None
            for k in range(layers):
                p, t, a = pbuf[k, where, cols], tbuf[k, where, cols], abuf[k, where, cols]
                index, upper = t & 7, t >= 8
                sat, shape, pore = (
                    jnp.where(upper, pick(tabs[i, 1], index), pick(tabs[i, 0], index)) for i in range(3)
                )
                wet = jnp.exp2(shape * jnp.minimum(p, 0.0))
                cond = sat * (wet * wet) * a.astype(jnp.float32)
                dry = pore * (1.0 - wet)
                water = pore * (1.0 / 0.85) - dry
                charge = cond * wet
                if k == 0:
                    c0[where, cols] = cond
                    total = (cond, dry, charge)
                else:
                    total = (total[0] + cond, total[1] + dry, total[2] + charge)
                    inner = flux(p_up, cond_up, p, cond)
                    moist[k - 1, where, cols] = water_up - inner
                    water = water + inner
                p_up, cond_up, water_up = p, cond, water
            moist[last, where, cols] = water_up
            c7[where, cols] = cond_up
            for q in range(3):
                part[chunk, block % 2, block // 2, q, :, half * LANES : (half + 1) * LANES] = total[q]

        @pl.loop(0, cols_all // tile)
        def _(block):
            for half in range(tile // LANES):
                lane_tile(block, half)

    @pl.loop(0, chunks + 1)
    def _(i):
        @pl.when(i < chunks)
        def _():
            column_pass((i + chunks - 1) % chunks)

        @pl.when(i == 0)
        def _():
            pl.semaphore_wait(barrier, 3 + (strip + strips - 1) // strips + (2 * strips - 2 - strip) // strips)

        @pl.when(i < chunks)
        def _():
            stage1((i + chunks - 1) % chunks).start()

        @pl.when(i > 0)
        def _():
            chunk = (i + chunks - 2) % chunks
            stage1(chunk).wait_recv()
            xs[chunk] = part[chunk, core, 1 - chip] + recv1[chunk, 1 - chip]
            stage2(chunk).start()

    def face(kind, e):
        where = pl.ds(pl.multiple_of(e * RE, RE), RE)
        src, dst, device = (
            (pbuf.at[last, where, part_a], dn_p.at[where], below),
            (c7.at[where, part_a], dn_c.at[where], below),
            (pbuf.at[0, where, part_b], up_p.at[where], above),
            (c0.at[where, part_b], up_c.at[where], above),
            (fb_out.at[where], fb_in.at[where], below),
            (fa_out.at[where], fa_in.at[where], above),
        )[kind]
        return remote(src, dst, face_send.at[kind, e], face_recv.at[kind, e], device)

    @pl.loop(0, edges)
    def _(e):
        @pl.when(has_down)
        def _():
            face(0, e).start()
            face(1, e).start()

        @pl.when(has_up)
        def _():
            face(2, e).start()
            face(3, e).start()

    for copy in small:
        copy.wait()

    @pl.when(depth == 0)
    def _():
        moist[0] = moist[0] + face_scale * rain[...]

    @pl.loop(0, chunks)
    def _(i):
        chunk = (i + chunks - 1) % chunks
        stage2(chunk).wait_recv()
        here = pl.ds(pl.multiple_of(chunk * R, R), R)
        there = pl.ds(pl.multiple_of(PAD + chunk * R, R), R)
        trans, store, charge = (
            (part[chunk, core, chip, q] + recv1[chunk, chip, q]) + recv2[chunk, q] for q in range(3)
        )
        store = spec_yield + store * layer_thick
        kind = code[here, :]
        river = jnp.where(kind == 1, river_cond, jnp.where(kind == 2, fixed_cond, 0.0))
        old = h0[here, :]
        E[0, there, mid] = trans * layer_thick
        E[1, there, mid] = store + river
        E[2, there, mid] = store * old + charge * (leak_rate * layer_thick) + river * sec[here, :]
        E[3, there, mid] = old

    lane = lax.broadcasted_iota(jnp.int32, (rows_all, LANES), 1) // 8

    def column_halo(side):
        return remote(
            colsend.at[side], colrecv.at[side], col_send.at[side], col_recv.at[side], (below, above)[side]
        )

    def pack(side):
        edge = pl.ds(LANES + (tile - LANES if side == 0 else 0), LANES)
        out = jnp.zeros((rows_all, LANES), jnp.float32)
        for q in range(4):
            shift = (8 * q + (8 if side == 0 else 0)) % LANES
            value = E[q, body, edge]
            out = jnp.where(lane == q, pltpu.roll(value, shift, 1) if shift else value, out)
        colsend[side] = out
        column_halo(side).start()

    def unpack(side):
        column_halo(side).wait_recv()
        value = colrecv[side]
        for q in range(4):
            shift = ((120 if side == 0 else LANES) - 8 * q) % LANES
            E[q, body, pl.ds(0 if side == 0 else LANES + tile, LANES)] = (
                pltpu.roll(value, shift, 1) if shift else value
            )

    def outside(side):
        for q in range(4):
            E[q, body, pl.ds(0 if side == 0 else LANES + tile, LANES)] = jnp.full(
                (rows_all, LANES), 1.0 if q == 1 else 0.0, jnp.float32
            )

    pl.when(has_down)(lambda: pack(0))
    pl.when(has_up)(lambda: pack(1))

    def face_step(e):
        where = pl.ds(pl.multiple_of(e * RE, RE), RE)

        @pl.when(has_down)
        def _():
            face(2, e).wait_recv()
            face(3, e).wait_recv()
            value = flux(pbuf[last, where, part_b], c7[where, part_b], up_p[where], up_c[where])
            fb_out[where] = value
            face(4, e).start()
            moist[last, where, part_b] = moist[last, where, part_b] - value

        @pl.when(has_up)
        def _():
            face(0, e).wait_recv()
            face(1, e).wait_recv()
            value = flux(dn_p[where], dn_c[where], pbuf[0, where, part_a], c0[where, part_a])
            fa_out[where] = value
            face(5, e).start()
            moist[0, where, part_a] = moist[0, where, part_a] + value

    pl.when(has_up)(lambda: unpack(0))
    pl.when(has_down)(lambda: unpack(1))
    pl.when(depth == 0)(lambda: outside(0))
    pl.when(depth == 3)(lambda: outside(1))

    def row_halo(side):
        mine = pl.ds(PAD if side == 0 else PAD + rows_all - 8, 8)
        theirs = pl.ds(PAD + rows_all if side == 0 else PAD - 8, 8)
        return remote(
            E.at[:, mine, :], E.at[:, theirs, :], row_send.at[side], row_recv.at[side], (north, south)[side]
        )

    pl.when(has_north)(lambda: row_halo(0).start())
    pl.when(has_south)(lambda: row_halo(1).start())

    for e in range(edges // 2):
        face_step(e)

    pl.when(has_south)(lambda: row_halo(0).wait_recv())
    pl.when(has_north)(lambda: row_halo(1).wait_recv())

    tiles = rows_all // 8 + 2
    sub = lax.broadcasted_iota(jnp.int32, (8, wide), 0)

    def rows_of(t):
        return pl.ds(pl.multiple_of(8 * t, 8), 8)

    def shift_down(ref, q, t):
        return jnp.where(sub == 0, pltpu.roll(ref[q, rows_of(t - 1), :], 1, 0), pltpu.roll(ref[q, rows_of(t), :], 1, 0))

    def shift_up(ref, q, t):
        return jnp.where(sub == 7, pltpu.roll(ref[q, rows_of(t + 1), :], 7, 0), pltpu.roll(ref[q, rows_of(t), :], 7, 0))

    @pl.loop(1, tiles + 1)
    def _(t):
        here = rows_of(t)
        trans = E[0, here, :]
        east = jnp.sqrt(trans * pltpu.roll(trans, wide - 1, 1))
        west = pltpu.roll(east, 1, 1)
        down = jnp.sqrt(trans * shift_up(E, 0, t))
        up = jnp.sqrt(trans * shift_down(E, 0, t))
        scale = 1.0 / (E[1, here, :] + east + west + down + up)
        C[0, here, :] = E[2, here, :] * scale
        C[1, here, :] = east * scale
        C[2, here, :] = west * scale
        C[3, here, :] = down * scale
        C[4, here, :] = up * scale

    for sweep in range(SWEEPS):
        src, q = (E, 3) if sweep == 0 else (H, (sweep - 1) % 2)

        @pl.loop(1, tiles + 1)
        def _(t):
            here = rows_of(t)
            value = src[q, here, :]
            H[sweep % 2, here, :] = (
                C[0, here, :]
                + C[1, here, :] * pltpu.roll(value, wide - 1, 1)
                + C[2, here, :] * pltpu.roll(value, 1, 1)
                + C[3, here, :] * shift_up(src, q, t)
                + C[4, here, :] * shift_down(src, q, t)
            )

    done = (SWEEPS - 1) % 2
    heads[depth] = H[done, body, mid]
    head[...] = H[done, body, mid]

    def send_head():
        return remote(heads.at[depth], heads.at[depth], head_send.at[0], head_recv.at[depth], {"depth": 3})

    pl.when(depth < 3)(lambda: send_head().start())

    for e in range(edges // 2, edges):
        face_step(e)

    @pl.loop(0, edges)
    def _(e):
        where = pl.ds(pl.multiple_of(e * RE, RE), RE)

        @pl.when(has_down)
        def _():
            face(5, e).wait_recv()
            moist[last, where, part_a] = moist[last, where, part_a] - fa_in[where]

        @pl.when(has_up)
        def _():
            face(4, e).wait_recv()
            moist[0, where, part_b] = moist[0, where, part_b] + fb_in[where]

    @pl.when(depth == 3)
    def _():
        for block in range(4):
            if block < 3:
                remote(heads.at[block], heads.at[block], head_send.at[0], head_recv.at[block], {"depth": 0}).wait_recv()
            cols = pl.ds(block * tile, tile)
            bottom = c7[:, cols] * (
                (pbuf[last, :, cols] - heads[block]) * (2.0 * face_scale / layer_thick) + face_scale
            )
            moist[last, :, cols] = moist[last, :, cols] - bottom

    @pl.loop(0, chunks)
    def _(i):
        stage1(i).wait_send()
        stage2(i).wait_send()

    @pl.loop(0, edges)
    def _(e):
        @pl.when(has_down)
        def _():
            for kind in (0, 1, 4):
                face(kind, e).wait_send()

        @pl.when(has_up)
        def _():
            for kind in (2, 3, 5):
                face(kind, e).wait_send()

    pl.when(has_down)(lambda: column_halo(0).wait_send())
    pl.when(has_up)(lambda: column_halo(1).wait_send())
    pl.when(has_north)(lambda: row_halo(0).wait_send())
    pl.when(has_south)(lambda: row_halo(1).wait_send())
    pl.when(depth < 3)(lambda: send_head().wait_send())


def shards(strips, pressure, texture, active, rain, k_sat, alpha, theta_sat, head_old, cell_code, section):
    layers, rows, cols = pressure.shape
    tile = head_old.shape[1]
    wide = tile + 2 * LANES
    cols_a = tile
    cols_b = cols - cols_a
    chunks, edges = rows // R, rows // RE
    f32 = jnp.float32
    vmem = lambda *shape: pltpu.VMEM(shape, f32)
    dma = lambda *shape: pltpu.SemaphoreType.DMA(shape)
    scratch = [
        vmem(layers, rows, cols),
        pltpu.VMEM((layers, rows, cols), jnp.int32),
        pltpu.VMEM((layers, rows, cols), jnp.int32),
        vmem(rows, cols),
        vmem(rows, tile),
        pltpu.VMEM((rows, tile), jnp.int32),
        vmem(rows, tile),
        vmem(3, 2, 8, LANES),
        vmem(chunks, 2, 2, 3, R, tile),
        vmem(chunks, 2, 3, R, tile),
        vmem(chunks, 3, R, tile),
        vmem(chunks, 3, R, tile),
        vmem(rows, cols),
        vmem(rows, cols),
        vmem(rows, cols_a),
        vmem(rows, cols_a),
        vmem(rows, cols_b),
        vmem(rows, cols_b),
        vmem(rows, cols_b),
        vmem(rows, cols_b),
        vmem(rows, cols_a),
        vmem(rows, cols_a),
        vmem(4, rows + 2 * PAD, wide),
        vmem(2, rows + 2 * PAD, wide),
        vmem(5, rows + 2 * PAD, wide),
        vmem(2, rows, LANES),
        vmem(2, rows, LANES),
        vmem(4, rows, tile),
        dma(3, chunks),
        dma(4),
        dma(chunks),
        dma(chunks),
        dma(chunks),
        dma(chunks),
        dma(6, edges),
        dma(6, edges),
        dma(2),
        dma(2),
        dma(2),
        dma(2),
        dma(1),
        dma(4),
    ]
    anywhere = pl.BlockSpec(memory_space=pltpu.HBM)
    return pl.pallas_call(
        functools.partial(kernel, strips),
        out_shape=(
            pltpu.VMEM((layers, rows, cols), f32),
            pltpu.VMEM((rows, tile), f32),
        ),
        in_specs=[pl.BlockSpec(memory_space=pltpu.SMEM)] * 3 + [anywhere] * 7,
        out_specs=(pl.BlockSpec(memory_space=pltpu.VMEM), pl.BlockSpec(memory_space=pltpu.VMEM)),
        scratch_shapes=scratch,
        compiler_params=pltpu.CompilerParams(
            collective_id=0, has_side_effects=True, vmem_limit_bytes=59 * 2**20
        ),
        name="soil_column",
    )(k_sat, alpha, theta_sat, pressure, texture, active, rain, head_old, cell_code, section)


def solution(mesh):
    in_specs = (
        P("depth", "strips", None),
        P("depth", "strips", None),
        P("depth", "strips", None),
        P("strips", None),
        P(),
        P(),
        P(),
        P("strips", "depth"),
        P("strips", "depth"),
        P("strips", "depth"),
    )
    out_specs = (P("depth", "strips", None), P("strips", "depth"))
    body = functools.partial(shards, mesh.shape["strips"])
    return jax.shard_map(body, mesh=mesh, in_specs=in_specs, out_specs=out_specs, check_vma=False)
```

time: 214 us -> 48.8 us (0.23); the launches traced: 211 us -> 48.7 us
  other arithmetic: 67.9 us -> 0 us
  waiting for transfers between devices: 64.3 us -> 0 us
  starting transfers between devices: 54.5 us -> 0 us
  Pallas kernels: 0 us -> 45.4 us
  between operations: 14.5 us -> 0.64 us
  blocking collectives: 6.5 us -> 0 us
    ppermute x18 -> x0, starting transfers between devices: 54.5 us -> none  [the longest x8 30.4 us: with_halo(): lax.ppermute(head, axis, [((i + 1) % count, i) for i in range(ends)])]
    pallas_call x0 -> x1, Pallas kernels: none -> 45.4 us  [shards(): pl.pallas_call(functools.partial(kernel, strips), out_shape=(pltpu.VMEM((...]
    reduce_sum x1 -> x0, other arithmetic: 40.2 us -> none  [shards(): trans_part = jnp.sum(conduct, axis=0)]
    psum x1 -> x0, waiting for transfers between devices: 32.8 us -> none  [shards(): summed = lax.psum((trans_part, store_part, charge_part), 'depth')]
    ppermute x18 -> x0, waiting for transfers between devices: 31.5 us -> none  [the longest x8 30.4 us: with_halo(): lax.ppermute(tail, axis, [(i, (i + 1) % count) for i in range(ends)])]
    eq x1 -> x0, other arithmetic: 9.72 us -> none  [lookup(): texture == class_id]
    mul x2 -> x0, other arithmetic: 8.17 us -> none  [the longest x1 7.25 us: face_flux(): return 0.5 * (cond_up + cond_low) * ((psi_up - psi_low) / layer_thick + 1.0)]
    all_gather x1 -> x0, blocking collectives: 6.5 us -> none  [shards(): full_head = lax.all_gather(head, 'depth', axis=1, tiled=True)]
  transfers between devices with their start and end apart: 19 -> 0, of which waited for: 8 -> 0; matrix products, arithmetic and copies ran while one was open for 5% -> 0% of each run, Pallas kernels for 0% -> 0%
where the time goes in v1:
time: 48.8 us; the launch traced here: 48.7 us
  Pallas kernels  45.4 us (93%)
  local copies, waits for them, and re-layouts  2.67 us (5%)
  between operations  0.64 us (1%)
    pallas_call x1, Pallas kernels, shards(): pl.pallas_call(functools.partial(kernel, strips), out_shape=(pltpu.VMEM((...  45.4 us
    unnamed x2, local copies, waits for them, and re-layouts  2.67 us

profile of v1, /device:TPU:104, one launch (start us, length us, event | category | flops | bytes accessed | tf_op | source)
XLA Modules:
  0.0 48.7 jit_solution(8758796440976550213)
XLA Ops:
  0.6 45.4 %soil_column.1 = (f32[8,128,1024]{2,1,0:T(8,128)S(1)}, f32[128,256]{1,0:T(8,128)S(1)}) custom-call(f32[12]{0:T(128)} %ks.1, f32[12]{0:T(128)} %al.1, f32[12]{0:T(128)} %th.1, f32[8,128,1024]{2,1,0:T(8,128)} %p_hbm.1, s32[8,128,1024]{2,1,0:T(8,128)} %t_hbm.1, s32[8,128,1024]{2,1,0:T(8,128)} %a_hbm.1, f32[128,1024]{1,0:T(8,128)} %rain_hbm.1, ...), custom_call_target="tpu_custom_call" | custom-call | tf_op jit(solution)/shard_map/soil_column/pallas_call | solution.py:489
  46.1 2.0 %copy.14 = f32[8,128,1024]{2,1,0:T(8,128)} copy(f32[8,128,1024]{2,1,0:T(8,128)S(1)} %get-tuple-element.2) | data formatting | bytes 8388608
  48.1 0.7 %copy.15 = f32[128,256]{1,0:T(8,128)} copy(f32[128,256]{1,0:T(8,128)S(1)} %get-tuple-element.3) | data formatting | bytes 262144

commit v2 on v1

--- a/solution.py
+++ b/solution.py
@@ -20,7 +20,8 @@
 face_scale = soil_step / layer_thick
 
 R = 16
-RE = 32
+RE = R
+LAG = 4
 PAD = 16
 LANES = 128
 
@@ -53,9 +54,9 @@
 
 
 def kernel(
-    strips, ks, al, th, p_hbm, t_hbm, a_hbm, rain_hbm, h_hbm, code_hbm, sec_hbm,
+    strips, ks_hbm, al_hbm, th_hbm, p_hbm, t_hbm, a_hbm, rain_hbm, h_hbm, code_hbm, sec_hbm,
     moist, head,
-    pbuf, tbuf, abuf, rain, h0, code, sec, tabs, part, recv1, xs, recv2, c0, c7,
+    ks, al, th, pbuf, tbuf, abuf, rain, h0, code, sec, tabs, part, recv1, xs, recv2, c0, c7,
     dn_p, dn_c, up_p, up_c, fb_out, fb_in, fa_out, fa_in,
     E, H, C, colsend, colrecv, heads,
     load_sem, misc_sem, s1_send, s1_recv, s2_send, s2_recv,
@@ -76,6 +77,7 @@
     cross = {"depth": (depth + 2) % 4}
     above, below = {"depth": depth - 1}, {"depth": depth + 1}
     north, south = {"strips": strip - 1}, {"strips": strip + 1}
+    early = edges // 3
     has_up, has_down = depth > 0, depth < 3
     has_north, has_south = strip > 0, strip < strips - 1
 
@@ -104,12 +106,20 @@
         pltpu.make_async_copy(src, dst, misc_sem.at[i])
         for i, (src, dst) in enumerate(((h_hbm, h0), (code_hbm, code), (sec_hbm, sec), (rain_hbm, rain)))
     ]
+    tables = [
+        pltpu.make_async_copy(src, dst, misc_sem.at[4 + i])
+        for i, (src, dst) in enumerate(((ks_hbm, ks), (al_hbm, al), (th_hbm, th)))
+    ]
+    for copy in tables:
+        copy.start()
     for i in range(chunks):
         for which in range(3):
             load(which, (i + chunks - 1) % chunks).start()
     for copy in small:
         copy.start()
 
+    for copy in tables:
+        copy.wait()
     scales = (1.0, 0.5 * math.log2(math.e), 0.85)
     row = lax.broadcasted_iota(jnp.int32, (8, LANES), 0)
     for i, (ref, scale) in enumerate(zip((ks, al, th), scales)):
@@ -131,9 +141,21 @@
     blank(PAD + rows_all + 8, 8)
     pl.when(strip == 0)(lambda: blank(8, 8))
     pl.when(strip == strips - 1)(lambda: blank(PAD + rows_all, 8))
-    for side in range(2):
+    for side in range(SWEEPS):
         H[side, 0:8, :] = jnp.zeros((8, wide), jnp.float32)
         H[side, 2 * PAD + rows_all - 8 :, :] = jnp.zeros((8, wide), jnp.float32)
+
+    def outside(side):
+        for q in range(4):
+            E[q, body, pl.ds(0 if side == 0 else LANES + tile, LANES)] = jnp.full(
+                (rows_all, LANES), 1.0 if q == 1 else 0.0, jnp.float32
+            )
+
+    pl.when(depth == 0)(lambda: outside(0))
+    pl.when(depth == 3)(lambda: outside(1))
+
+    def order(i):
+        return (i + chunks - 1) % chunks
 
     def stage1(chunk):
         return remote(
@@ -181,61 +203,19 @@
             for half in range(tile // LANES):
                 lane_tile(block, half)
 
-    @pl.loop(0, chunks + 1)
-    def _(i):
-        @pl.when(i < chunks)
-        def _():
-            column_pass((i + chunks - 1) % chunks)
-
-        @pl.when(i == 0)
-        def _():
-            pl.semaphore_wait(barrier, 3 + (strip + strips - 1) // strips + (2 * strips - 2 - strip) // strips)
-
-        @pl.when(i < chunks)
-        def _():
-            stage1((i + chunks - 1) % chunks).start()
-
-        @pl.when(i > 0)
-        def _():
-            chunk = (i + chunks - 2) % chunks
-            stage1(chunk).wait_recv()
-            xs[chunk] = part[chunk, core, 1 - chip] + recv1[chunk, 1 - chip]
-            stage2(chunk).start()
-
     def face(kind, e):
         where = pl.ds(pl.multiple_of(e * RE, RE), RE)
         src, dst, device = (
-            (pbuf.at[last, where, part_a], dn_p.at[where], below),
+            (p_hbm.at[last, where, part_a], dn_p.at[where], below),
             (c7.at[where, part_a], dn_c.at[where], below),
-            (pbuf.at[0, where, part_b], up_p.at[where], above),
+            (p_hbm.at[0, where, part_b], up_p.at[where], above),
             (c0.at[where, part_b], up_c.at[where], above),
             (fb_out.at[where], fb_in.at[where], below),
             (fa_out.at[where], fa_in.at[where], above),
         )[kind]
         return remote(src, dst, face_send.at[kind, e], face_recv.at[kind, e], device)
 
-    @pl.loop(0, edges)
-    def _(e):
-        @pl.when(has_down)
-        def _():
-            face(0, e).start()
-            face(1, e).start()
-
-        @pl.when(has_up)
-        def _():
-            face(2, e).start()
-            face(3, e).start()
-
-    for copy in small:
-        copy.wait()
-
-    @pl.when(depth == 0)
-    def _():
-        moist[0] = moist[0] + face_scale * rain[...]
-
-    @pl.loop(0, chunks)
-    def _(i):
-        chunk = (i + chunks - 1) % chunks
+    def finish(chunk):
         stage2(chunk).wait_recv()
         here = pl.ds(pl.multiple_of(chunk * R, R), R)
         there = pl.ds(pl.multiple_of(PAD + chunk * R, R), R)
@@ -250,67 +230,42 @@
         E[1, there, mid] = store + river
         E[2, there, mid] = store * old + charge * (leak_rate * layer_thick) + river * sec[here, :]
         E[3, there, mid] = old
-
-    lane = lax.broadcasted_iota(jnp.int32, (rows_all, LANES), 1) // 8
-
-    def column_halo(side):
+        pl.when(has_down)(lambda: pack(0, chunk))
+        pl.when(has_up)(lambda: pack(1, chunk))
+
+    lane = lax.broadcasted_iota(jnp.int32, (R, LANES), 1) // 8
+
+    def column_halo(side, chunk):
+        where = pl.ds(pl.multiple_of(chunk * R, R), R)
         return remote(
-            colsend.at[side], colrecv.at[side], col_send.at[side], col_recv.at[side], (below, above)[side]
-        )
-
-    def pack(side):
+            colsend.at[side, where], colrecv.at[side, where],
+            col_send.at[side, chunk], col_recv.at[side, chunk], (below, above)[side],
+        )
+
+    def pack(side, chunk):
         edge = pl.ds(LANES + (tile - LANES if side == 0 else 0), LANES)
-        out = jnp.zeros((rows_all, LANES), jnp.float32)
+        there = pl.ds(pl.multiple_of(PAD + chunk * R, R), R)
+        out = jnp.zeros((R, LANES), jnp.float32)
         for q in range(4):
             shift = (8 * q + (8 if side == 0 else 0)) % LANES
-            value = E[q, body, edge]
+            value = E[q, there, edge]
             out = jnp.where(lane == q, pltpu.roll(value, shift, 1) if shift else value, out)
-        colsend[side] = out
-        column_halo(side).start()
-
-    def unpack(side):
-        column_halo(side).wait_recv()
-        value = colrecv[side]
+        colsend[side, pl.ds(pl.multiple_of(chunk * R, R), R)] = out
+        column_halo(side, chunk).start()
+
+    def unpack_side(side, chunk):
+        there = pl.ds(pl.multiple_of(PAD + chunk * R, R), R)
+        column_halo(side, chunk).wait_recv()
+        value = colrecv[side, pl.ds(pl.multiple_of(chunk * R, R), R)]
         for q in range(4):
             shift = ((120 if side == 0 else LANES) - 8 * q) % LANES
-            E[q, body, pl.ds(0 if side == 0 else LANES + tile, LANES)] = (
+            E[q, there, pl.ds(0 if side == 0 else LANES + tile, LANES)] = (
                 pltpu.roll(value, shift, 1) if shift else value
             )
 
-    def outside(side):
-        for q in range(4):
-            E[q, body, pl.ds(0 if side == 0 else LANES + tile, LANES)] = jnp.full(
-                (rows_all, LANES), 1.0 if q == 1 else 0.0, jnp.float32
-            )
-
-    pl.when(has_down)(lambda: pack(0))
-    pl.when(has_up)(lambda: pack(1))
-
-    def face_step(e):
-        where = pl.ds(pl.multiple_of(e * RE, RE), RE)
-
-        @pl.when(has_down)
-        def _():
-            face(2, e).wait_recv()
-            face(3, e).wait_recv()
-            value = flux(pbuf[last, where, part_b], c7[where, part_b], up_p[where], up_c[where])
-            fb_out[where] = value
-            face(4, e).start()
-            moist[last, where, part_b] = moist[last, where, part_b] - value
-
-        @pl.when(has_up)
-        def _():
-            face(0, e).wait_recv()
-            face(1, e).wait_recv()
-            value = flux(dn_p[where], dn_c[where], pbuf[0, where, part_a], c0[where, part_a])
-            fa_out[where] = value
-            face(5, e).start()
-            moist[0, where, part_a] = moist[0, where, part_a] + value
-
-    pl.when(has_up)(lambda: unpack(0))
-    pl.when(has_down)(lambda: unpack(1))
-    pl.when(depth == 0)(lambda: outside(0))
-    pl.when(depth == 3)(lambda: outside(1))
+    def unpack(chunk):
+        pl.when(has_up)(lambda: unpack_side(0, chunk))
+        pl.when(has_down)(lambda: unpack_side(1, chunk))
 
     def row_halo(side):
         mine = pl.ds(PAD if side == 0 else PAD + rows_all - 8, 8)
@@ -319,16 +274,88 @@
             E.at[:, mine, :], E.at[:, theirs, :], row_send.at[side], row_recv.at[side], (north, south)[side]
         )
 
-    pl.when(has_north)(lambda: row_halo(0).start())
-    pl.when(has_south)(lambda: row_halo(1).start())
-
-    for e in range(edges // 2):
-        face_step(e)
-
-    pl.when(has_south)(lambda: row_halo(0).wait_recv())
-    pl.when(has_north)(lambda: row_halo(1).wait_recv())
-
-    tiles = rows_all // 8 + 2
+    @pl.loop(0, chunks + 1)
+    def _(i):
+        @pl.when(i < chunks)
+        def _():
+            column_pass(order(i))
+
+        @pl.when(i == 0)
+        def _():
+            pl.semaphore_wait(barrier, 3 + (strip + strips - 1) // strips + (2 * strips - 2 - strip) // strips)
+
+            @pl.loop(0, edges)
+            def _(e):
+                pl.when(has_down)(lambda: face(0, e).start())
+
+            @pl.loop(0, early)
+            def _(e):
+                pl.when(has_up)(lambda: face(2, e).start())
+
+            for copy in small:
+                copy.wait()
+
+        @pl.when(i > 0)
+        def _():
+            chunk = order(i - 1)
+            stage1(chunk).wait_recv()
+            xs[chunk] = part[chunk, core, 1 - chip] + recv1[chunk, 1 - chip]
+
+        @pl.when(i < chunks)
+        def _():
+            stage1(order(i)).start()
+
+        @pl.when(i > 0)
+        def _():
+            stage2(order(i - 1)).start()
+
+        @pl.when(i >= LAG)
+        def _():
+            finish(order(i - LAG))
+
+        @pl.when(i == LAG + 3)
+        def _():
+            unpack(chunks - 1)
+            unpack(0)
+            pl.when(has_north)(lambda: row_halo(0).start())
+            pl.when(has_south)(lambda: row_halo(1).start())
+
+    @pl.loop(0, edges)
+    def _(e):
+        @pl.when(has_down)
+        def _():
+            face(1, e).start()
+
+        @pl.when(has_up)
+        def _():
+            pl.when(e >= early)(lambda: face(2, e).start())
+            face(3, e).start()
+
+    @pl.when(depth == 0)
+    def _():
+        moist[0] = moist[0] + face_scale * rain[...]
+
+    def face_step(e):
+        where = pl.ds(pl.multiple_of(e * RE, RE), RE)
+
+        @pl.when(has_down)
+        def _():
+            face(2, e).wait_recv()
+            face(3, e).wait_recv()
+            value = flux(pbuf[last, where, part_b], c7[where, part_b], up_p[where], up_c[where])
+            fb_out[where] = value
+            moist[last, where, part_b] = moist[last, where, part_b] - value
+            face(4, e).start()
+
+        @pl.when(has_up)
+        def _():
+            face(0, e).wait_recv()
+            face(1, e).wait_recv()
+            value = flux(dn_p[where], dn_c[where], pbuf[0, where, part_a], c0[where, part_a])
+            fa_out[where] = value
+            moist[0, where, part_a] = moist[0, where, part_a] + value
+            face(5, e).start()
+
     sub = lax.broadcasted_iota(jnp.int32, (8, wide), 0)
 
     def rows_of(t):
@@ -340,8 +367,7 @@
     def shift_up(ref, q, t):
         return jnp.where(sub == 7, pltpu.roll(ref[q, rows_of(t + 1), :], 7, 0), pltpu.roll(ref[q, rows_of(t), :], 7, 0))
 
-    @pl.loop(1, tiles + 1)
-    def _(t):
+    def coefficients(t):
         here = rows_of(t)
         trans = E[0, here, :]
         east = jnp.sqrt(trans * pltpu.roll(trans, wide - 1, 1))
@@ -355,37 +381,97 @@
         C[3, here, :] = down * scale
         C[4, here, :] = up * scale
 
-    for sweep in range(SWEEPS):
-        src, q = (E, 3) if sweep == 0 else (H, (sweep - 1) % 2)
-
-        @pl.loop(1, tiles + 1)
-        def _(t):
-            here = rows_of(t)
-            value = src[q, here, :]
-            H[sweep % 2, here, :] = (
-                C[0, here, :]
-                + C[1, here, :] * pltpu.roll(value, wide - 1, 1)
-                + C[2, here, :] * pltpu.roll(value, 1, 1)
-                + C[3, here, :] * shift_up(src, q, t)
-                + C[4, here, :] * shift_down(src, q, t)
-            )
-
-    done = (SWEEPS - 1) % 2
-    heads[depth] = H[done, body, mid]
-    head[...] = H[done, body, mid]
-
-    def send_head():
-        return remote(heads.at[depth], heads.at[depth], head_send.at[0], head_recv.at[depth], {"depth": 3})
-
-    pl.when(depth < 3)(lambda: send_head().start())
-
-    for e in range(edges // 2, edges):
+    def sweep(n, t):
+        src, q = (E, 3) if n == 0 else (H, n - 1)
+        here = rows_of(t)
+        value = src[q, here, :]
+        H[n, here, :] = (
+            C[0, here, :]
+            + C[1, here, :] * pltpu.roll(value, wide - 1, 1)
+            + C[2, here, :] * pltpu.roll(value, 1, 1)
+            + C[3, here, :] * shift_up(src, q, t)
+            + C[4, here, :] * shift_down(src, q, t)
+        )
+
+    tiles = rows_all // 8 + 2
+
+    def wave(t, first=0, final=False):
+        if not final:
+            coefficients(t)
+            sweep(0, t)
+        for n in range(1, SWEEPS):
+            if first == 0 or t - n >= n:
+                sweep(n, t - n)
+
+    def head_copy(chunk, source):
+        where = pl.ds(pl.multiple_of(chunk * R, R), R)
+        return remote(
+            heads.at[source, where], heads.at[source, where],
+            head_send.at[chunk], head_recv.at[source, chunk], {"depth": 3},
+        )
+
+    def hand_on(chunk):
+        where = pl.ds(pl.multiple_of(chunk * R, R), R)
+        value = H[SWEEPS - 1, pl.ds(pl.multiple_of(PAD + chunk * R, R), R), mid]
+        heads[depth, where] = value
+        head[where, :] = value
+        pl.when(depth < 3)(lambda: head_copy(chunk, depth).start())
+
+    for i in range(chunks + 1 - LAG, chunks):
+        finish((i + chunks - 1) % chunks)
+    for i in range(2, 5):
+        unpack((i + chunks - 1) % chunks)
+
+    pl.when(has_south)(lambda: row_halo(0).wait_recv())
+    pl.when(has_north)(lambda: row_halo(1).wait_recv())
+
+    for t in (1, 2, 3):
+        wave(t, first=1)
+    wave(4)
+
+    @pl.loop(2, 4)
+    def _(chunk):
+        wave(2 * chunk + 1)
+        wave(2 * chunk + 2)
+        hand_on(chunk - 2)
+
+    face_step(0)
+    face_step(1)
+
+    @pl.loop(4, chunks - 1)
+    def _(chunk):
+        unpack(chunk)
+        wave(2 * chunk + 1)
+        wave(2 * chunk + 2)
+        hand_on(chunk - 2)
+        face_step(chunk - 2)
+
+    for t in range(tiles - 3, tiles + 1):
+        wave(t)
+    hand_on(chunks - 3)
+    hand_on(chunks - 2)
+    wave(tiles + 1, final=True)
+    hand_on(chunks - 1)
+
+    @pl.loop(chunks - 3, edges)
+    def _(e):
         face_step(e)
 
     @pl.loop(0, edges)
     def _(e):
         where = pl.ds(pl.multiple_of(e * RE, RE), RE)
 
+        @pl.when(depth == 3)
+        def _():
+            for block in range(4):
+                if block < 3:
+                    head_copy(e, block).wait_recv()
+                cols = pl.ds(block * tile, tile)
+                bottom = c7[where, cols] * (
+                    (pbuf[last, where, cols] - heads[block, where]) * (2.0 * face_scale / layer_thick) + face_scale
+                )
+                moist[last, where, cols] = moist[last, where, cols] - bottom
+
         @pl.when(has_down)
         def _():
             face(5, e).wait_recv()
@@ -395,40 +481,37 @@
         def _():
             face(4, e).wait_recv()
             moist[0, where, part_b] = moist[0, where, part_b] + fb_in[where]
-
-    @pl.when(depth == 3)
-    def _():
-        for block in range(4):
-            if block < 3:
-                remote(heads.at[block], heads.at[block], head_send.at[0], head_recv.at[block], {"depth": 0}).wait_recv()
-            cols = pl.ds(block * tile, tile)
-            bottom = c7[:, cols] * (
-                (pbuf[last, :, cols] - heads[block]) * (2.0 * face_scale / layer_thick) + face_scale
-            )
-            moist[last, :, cols] = moist[last, :, cols] - bottom
 
     @pl.loop(0, chunks)
     def _(i):
         stage1(i).wait_send()
         stage2(i).wait_send()
 
-    @pl.loop(0, edges)
-    def _(e):
         @pl.when(has_down)
         def _():
             for kind in (0, 1, 4):
-                face(kind, e).wait_send()
+                face(kind, i).wait_send()
+            column_halo(0, i).wait_send()
+            head_copy(i, depth).wait_send()
 
         @pl.when(has_up)
         def _():
             for kind in (2, 3, 5):
-                face(kind, e).wait_send()
-
-    pl.when(has_down)(lambda: column_halo(0).wait_send())
-    pl.when(has_up)(lambda: column_halo(1).wait_send())
+                face(kind, i).wait_send()
+            column_halo(1, i).wait_send()
+
     pl.when(has_north)(lambda: row_halo(0).wait_send())
     pl.when(has_south)(lambda: row_halo(1).wait_send())
-    pl.when(depth < 3)(lambda: send_head().wait_send())
+
+
+def store_kernel(moist, head, moist_out, head_out, sems):
+    copies = [pltpu.make_async_copy(head, head_out, sems.at[0])]
+    for k in range(moist.shape[0]):
+        copies.append(pltpu.make_async_copy(moist.at[k], moist_out.at[k], sems.at[k + 1]))
+    for copy in copies:
+        copy.start()
+    for copy in copies:
+        copy.wait()
 
 
 def shards(strips, pressure, texture, active, rain, k_sat, alpha, theta_sat, head_old, cell_code, section):
@@ -441,7 +524,11 @@
     f32 = jnp.float32
     vmem = lambda *shape: pltpu.VMEM(shape, f32)
     dma = lambda *shape: pltpu.SemaphoreType.DMA(shape)
+    table = pltpu.SMEM(k_sat.shape, f32)
     scratch = [
+        table,
+        table,
+        table,
         vmem(layers, rows, cols),
         pltpu.VMEM((layers, rows, cols), jnp.int32),
         pltpu.VMEM((layers, rows, cols), jnp.int32),
@@ -465,34 +552,34 @@
         vmem(rows, cols_a),
         vmem(rows, cols_a),
         vmem(4, rows + 2 * PAD, wide),
-        vmem(2, rows + 2 * PAD, wide),
+        vmem(SWEEPS, rows + 2 * PAD, wide),
         vmem(5, rows + 2 * PAD, wide),
         vmem(2, rows, LANES),
         vmem(2, rows, LANES),
         vmem(4, rows, tile),
         dma(3, chunks),
-        dma(4),
+        dma(7),
         dma(chunks),
         dma(chunks),
         dma(chunks),
         dma(chunks),
         dma(6, edges),
         dma(6, edges),
+        dma(2, chunks),
+        dma(2, chunks),
         dma(2),
         dma(2),
-        dma(2),
-        dma(2),
-        dma(1),
-        dma(4),
+        dma(chunks),
+        dma(4, chunks),
     ]
     anywhere = pl.BlockSpec(memory_space=pltpu.HBM)
-    return pl.pallas_call(
+    moist, head = pl.pallas_call(
         functools.partial(kernel, strips),
         out_shape=(
             pltpu.VMEM((layers, rows, cols), f32),
             pltpu.VMEM((rows, tile), f32),
         ),
-        in_specs=[pl.BlockSpec(memory_space=pltpu.SMEM)] * 3 + [anywhere] * 7,
+        in_specs=[anywhere] * 10,
         out_specs=(pl.BlockSpec(memory_space=pltpu.VMEM), pl.BlockSpec(memory_space=pltpu.VMEM)),
         scratch_shapes=scratch,
         compiler_params=pltpu.CompilerParams(
@@ -500,6 +587,19 @@
         ),
         name="soil_column",
     )(k_sat, alpha, theta_sat, pressure, texture, active, rain, head_old, cell_code, section)
+    on_chip = pl.BlockSpec(memory_space=pltpu.VMEM)
+    return pl.pallas_call(
+        store_kernel,
+        out_shape=(
+            jax.ShapeDtypeStruct((layers, rows, cols), f32),
+            jax.ShapeDtypeStruct((rows, tile), f32),
+        ),
+        in_specs=[on_chip] * 2,
+        out_specs=(anywhere, anywhere),
+        scratch_shapes=[dma(layers + 1)],
+        compiler_params=pltpu.CompilerParams(vmem_limit_bytes=2**20),
+        name="store",
+    )(pltpu.with_memory_space_constraint(moist, pltpu.VMEM), pltpu.with_memory_space_constraint(head, pltpu.VMEM))
 
 
 def solution(mesh):

time: 48.8 us -> 37.6 us (0.77)
  Pallas kernels: 45.4 us -> 36.8 us
  local copies, waits for them, and re-layouts: 2.67 us -> 0 us
    pallas_call x1, Pallas kernels: 45.4 us -> 34.7 us  [shards(): pl.pallas_call(functools.partial(kernel, strips), out_shape=(pltpu.VMEM((...]
    unnamed x2 -> x0, local copies, waits for them, and re-layouts: 2.67 us -> none
    pallas_call x0 -> x1, Pallas kernels: none -> 2.12 us  [shards(): pl.pallas_call(store_kernel, out_shape=(jax.ShapeDtypeStruct((layers, row...]
where the time goes in v2:
time: 37.6 us; the launch traced here: 37.5 us
  Pallas kernels  36.8 us (98%)
  between operations  0.64 us (2%)
    pallas_call x1, Pallas kernels, shards(): pl.pallas_call(functools.partial(kernel, strips), out_shape=(pltpu.VMEM((...  34.7 us
    pallas_call x1, Pallas kernels, shards(): pl.pallas_call(store_kernel, out_shape=(jax.ShapeDtypeStruct((layers, row...  2.12 us

profile of v2, /device:TPU:104, one launch (start us, length us, event | category | flops | bytes accessed | tf_op | source)
XLA Modules:
  0.0 37.5 jit_solution(1814165632502964864)
XLA Ops:
  0.6 34.7 %soil_column.1 = (f32[8,128,1024]{2,1,0:T(8,128)S(1)}, f32[128,256]{1,0:T(8,128)S(1)}) custom-call(f32[12]{0:T(128)} %ks_hbm.1, f32[12]{0:T(128)} %al_hbm.1, f32[12]{0:T(128)} %th_hbm.1, f32[8,128,1024]{2,1,0:T(8,128)} %p_hbm.1, s32[8,128,1024]{2,1,0:T(8,128)} %t_hbm.1, s32[8,128,1024]{2,1,0:T(8,128)} %a_hbm.1, f32[128,1024]{1,0:T(8,128)} %rain_hbm.1, ...), custom_call_target="tpu_custom_call" | custom-call | tf_op jit(solution)/shard_map/soil_column/pallas_call | solution.py:576
  35.4 2.1 %store.1 = (f32[8,128,1024]{2,1,0:T(8,128)}, f32[128,256]{1,0:T(8,128)}) custom-call(f32[8,128,1024]{2,1,0:T(8,128)S(1)} %get-tuple-element.4.moist, f32[128,256]{1,0:T(8,128)S(1)} %get-tuple-element.5.head), custom_call_target="tpu_custom_call" | custom-call | tf_op jit(solution)/shard_map/store/pallas_call | solution.py:591

commit v3 on v2

v3 whole, which is shorter than its diff:
```python
import functools
import math

import jax
import jax.numpy as jnp
from jax import lax
from jax.experimental import pallas as pl
from jax.experimental.pallas import tpu as pltpu
from jax.sharding import PartitionSpec as P

MESH = pl.DeviceIdType.MESH
SWEEPS = 3

layer_thick = 0.05
soil_step = 0.0002
spec_yield = 0.02
leak_rate = 0.5
river_cond = 0.5
fixed_cond = 3.0
face_scale = soil_step / layer_thick

R = 16
RE = R
PAD = 24
LANES = 128


def pick(table, index):
    dims = lax.GatherDimensionNumbers(
        offset_dims=(),
        collapsed_slice_dims=(0,),
        start_index_map=(0,),
        operand_batching_dims=(1,),
        start_indices_batching_dims=(1,),
    )
    rows = [
        lax.gather(
            table,
            index[8 * i : 8 * i + 8, :, None],
            dims,
            slice_sizes=(1, 1),
            mode=lax.GatherScatterMode.PROMISE_IN_BOUNDS,
        )
        for i in range(index.shape[0] // 8)
    ]
    return jnp.concatenate(rows, axis=0)


def flux(psi_up, cond_up, psi_low, cond_low):
    return (cond_up + cond_low) * (
        (psi_up - psi_low) * (0.5 * face_scale / layer_thick) + 0.5 * face_scale
    )


def kernel(
    strips, ks_hbm, al_hbm, th_hbm, p_hbm, t_hbm, a_hbm, rain_hbm, h_hbm, code_hbm, sec_hbm,
    moist, head,
    ks, al, th, pbuf, tbuf, abuf, rain, h0, code, sec, tabs, part, recv1, xs, recv2, c0, c7,
    dn_p, dn_c, up_pc, fb_out, fb_in, fa_out, fa_in,
    E, H, A, colsend, colrecv, heads,
    load_sem, misc_sem, s1_send, s1_recv, s2_send, s2_recv,
    face_send, down_recv, up_recv, fb_recv, fa_recv, col_send, col_recv, row_send, row_recv, head_send, head_recv,
):
    layers, rows_all, cols_all = pbuf.shape
    chunks, edges = rows_all // R, rows_all // RE
    tile = h0.shape[1]
    wide = tile + LANES
    cols_a = dn_p.shape[1]
    part_a, part_b = pl.ds(0, cols_a), pl.ds(cols_a, cols_all - cols_a)
    body = pl.ds(PAD, rows_all)
    mid, halo = pl.ds(0, tile), pl.ds(tile, LANES)
    last = layers - 1
    depth, strip = lax.axis_index("depth"), lax.axis_index("strips")
    core, chip = depth % 2, depth // 2
    mate = {"depth": chip * 2 + 1 - core}
    cross = {"depth": (depth + 2) % 4}
    above, below = {"depth": depth - 1}, {"depth": depth + 1}
    north, south = {"strips": strip - 1}, {"strips": strip + 1}
    early = edges // 3
    has_up, has_down = depth > 0, depth < 3
    has_north, has_south = strip > 0, strip < strips - 1

    def remote(src, dst, send, recv, device):
        return pltpu.make_async_remote_copy(
            src_ref=src, dst_ref=dst, send_sem=send, recv_sem=recv,
            device_id=device, device_id_type=MESH,
        )

    barrier = pltpu.get_barrier_semaphore()

    def greet(device):
        pl.semaphore_signal(barrier, inc=1, device_id=device, device_id_type=MESH)

    for step in (1, 2, 3):
        greet({"depth": (depth + step) % 4})
    pl.when(has_north)(lambda: greet(north))
    pl.when(has_south)(lambda: greet(south))

    def load(which, chunk):
        src, dst = ((p_hbm, pbuf), (t_hbm, tbuf), (a_hbm, abuf))[which]
        where = pl.ds(pl.multiple_of(chunk * R, R), R)
        return pltpu.make_async_copy(src.at[:, where, :], dst.at[:, where, :], load_sem.at[which, chunk])

    small = [
        pltpu.make_async_copy(src, dst, misc_sem.at[i])
        for i, (src, dst) in enumerate(((h_hbm, h0), (code_hbm, code), (sec_hbm, sec), (rain_hbm, rain)))
    ]
    tables = [
        pltpu.make_async_copy(src, dst, misc_sem.at[4 + i])
        for i, (src, dst) in enumerate(((ks_hbm, ks), (al_hbm, al), (th_hbm, th)))
    ]
    for copy in tables:
        copy.start()
    for i in range(chunks):
        for which in range(3):
            load(which, (i + chunks - 1) % chunks).start()
    for copy in small:
        copy.start()

    for copy in tables:
        copy.wait()
    scales = (1.0, 0.5 * math.log2(math.e), 0.85)
    row = lax.broadcasted_iota(jnp.int32, (8, LANES), 0)
    for i, (ref, scale) in enumerate(zip((ks, al, th), scales)):
        low = high = jnp.zeros((8, LANES), jnp.float32)
        for c in range(ref.shape[0]):
            value = ref[c] * scale
            if c < 8:
                low = jnp.where(row == c, value, low)
            else:
                high = jnp.where(row == c - 8, value, high)
        tabs[i, 0] = low
        tabs[i, 1] = high

    def blank(first, count):
        for q in range(4):
            E[q, first : first + count, :] = jnp.full((count, wide), 1.0 if q == 1 else 0.0, jnp.float32)

    blank(0, PAD - 8)
    blank(PAD + rows_all + 8, PAD - 8)
    pl.when(strip == 0)(lambda: blank(PAD - 8, 8))
    pl.when(strip == strips - 1)(lambda: blank(PAD + rows_all, 8))
    for ref in (A, H):
        for q in range(ref.shape[0]):
            ref[q, 0:PAD, :] = jnp.zeros((PAD, wide), jnp.float32)
            ref[q, PAD + rows_all :, :] = jnp.zeros((PAD, wide), jnp.float32)

    def outside(side):
        group = lax.broadcasted_iota(jnp.int32, (8, LANES), 1) // 8
        for chunk in range(chunks + 1):
            colrecv[side, chunk] = jnp.where(group % 4 == 1, 1.0, 0.0)

    pl.when(depth == 0)(lambda: outside(0))
    pl.when(depth == 3)(lambda: outside(1))

    def order(i):
        return (i + chunks - 1) % chunks

    def stage1(chunk):
        return remote(
            part.at[chunk, 1 - core], recv1.at[chunk], s1_send.at[0], s1_recv.at[chunk], mate
        )

    def stage2(chunk):
        return remote(xs.at[chunk], recv2.at[chunk], s2_send.at[0], s2_recv.at[chunk], cross)

    def column_pass(chunk):
        for which in range(3):
            load(which, chunk).wait()
        where = pl.ds(pl.multiple_of(chunk * R, R), R)

        def lane_tile(block, half):
            cols = pl.ds(pl.multiple_of(block * tile + half * LANES, LANES), LANES)
            total = None
            for k in range(layers):
                p, t, a = pbuf[k, where, cols], tbuf[k, where, cols], abuf[k, where, cols]
                index, upper = t & 7, t >= 8
                sat, shape, pore = (
                    jnp.where(upper, pick(tabs[i, 1], index), pick(tabs[i, 0], index)) for i in range(3)
                )
                wet = jnp.exp2(shape * jnp.minimum(p, 0.0))
                cond = sat * (wet * wet) * a.astype(jnp.float32)
                dry = pore * (1.0 - wet)
                water = pore * (1.0 / 0.85) - dry
                charge = cond * wet
                if k == 0:
                    c0[where, cols] = cond
                    total = (cond, dry, charge)
                else:
                    total = (total[0] + cond, total[1] + dry, total[2] + charge)
                    inner = flux(p_up, cond_up, p, cond)
                    moist[k - 1, where, cols] = water_up - inner
                    water = water + inner
                p_up, cond_up, water_up = p, cond, water
            moist[last, where, cols] = water_up
            c7[where, cols] = cond_up
            for q in range(3):
                part[chunk, block % 2, block // 2, q, :, half * LANES : (half + 1) * LANES] = total[q]

        @pl.loop(0, cols_all // tile)
        def _(block):
            for half in range(tile // LANES):
                lane_tile(block, half)

    half = rows_all // 2

    def down_p():
        return remote(p_hbm.at[last, :, part_a], dn_p, face_send.at[0], down_recv.at[0], below)

    def down_c(k):
        where = pl.ds(k * half, half)
        return remote(c7.at[where, part_a], dn_c.at[where], face_send.at[1], down_recv.at[1 + k], below)

    def up_message(which, e):
        where = pl.ds(pl.multiple_of(e * RE, RE), RE)
        src = p_hbm.at[0, where, part_b] if which == 0 else c0.at[where, part_b]
        return remote(src, up_pc.at[e, which], face_send.at[2 + which], up_recv.at[e], above)

    def flux_down(e):
        where = pl.ds(pl.multiple_of(e * RE, RE), RE)
        return remote(fb_out.at[where], fb_in.at[where], face_send.at[4], fb_recv.at[e], below)

    def flux_up(e):
        where = pl.ds(pl.multiple_of(e * RE, RE), RE)
        return remote(fa_out.at[where], fa_in.at[where], face_send.at[5], fa_recv.at[0], above)

    def finish(chunk):
        stage2(chunk).wait_recv()
        here = pl.ds(pl.multiple_of(chunk * R, R), R)
        there = pl.ds(pl.multiple_of(PAD + chunk * R, 8), R)
        trans, store, charge = (
            (part[chunk, core, chip, q] + recv1[chunk, chip, q]) + recv2[chunk, q] for q in range(3)
        )
        store = spec_yield + store * layer_thick
        kind = code[here, :]
        river = jnp.where(kind == 1, river_cond, jnp.where(kind == 2, fixed_cond, 0.0))
        old = h0[here, :]
        root = jnp.sqrt(trans * layer_thick)
        E[0, there, mid] = root
        E[1, there, mid] = store + river
        E[2, there, mid] = store * old + charge * (leak_rate * layer_thick) + river * sec[here, :]
        E[3, there, mid] = root * old
        pack(chunk, tiles_of(chunk))

    lane = lax.broadcasted_iota(jnp.int32, (8, LANES), 1) // 8

    def column_halo(side, chunk):
        return remote(
            colsend.at[side, chunk], colrecv.at[side, chunk],
            col_send.at[side], col_recv.at[side, chunk], (below, above)[side],
        )

    def pack_tiles(side, chunk, tiles):
        edge = pl.ds(tile - LANES if side == 0 else 0, LANES)
        out = jnp.zeros((8, LANES), jnp.float32)
        for q in range(4):
            for h in range(2):
                group = q + 4 * h
                shift = (8 * group + (8 if side == 0 else 0)) % LANES
                value = E[q, tiles[h], edge]
                out = jnp.where(lane == group, pltpu.roll(value, shift, 1) if shift else value, out)
        colsend[side, chunk] = out
        column_halo(side, chunk).start()

    def tiles_of(chunk):
        return [pl.ds(pl.multiple_of(PAD + chunk * R + 8 * h, 8), 8) for h in range(2)]

    halo_tiles = [pl.ds(PAD - 8, 8), pl.ds(PAD + rows_all, 8)]

    def pack(chunk, tiles):
        pl.when(has_down)(lambda: pack_tiles(0, chunk, tiles))
        pl.when(has_up)(lambda: pack_tiles(1, chunk, tiles))

    def unpack(chunk, tiles=None):
        pl.when(has_up)(lambda: column_halo(0, chunk).wait_recv())
        pl.when(has_down)(lambda: column_halo(1, chunk).wait_recv())
        west, east = colrecv[0, chunk], colrecv[1, chunk]
        for q in range(4):
            for h in range(2):
                group = q + 4 * h
                moved = pltpu.roll(west, 120 - 8 * group, 1)
                E[q, (tiles or tiles_of(chunk))[h], halo] = jnp.where(
                    lane < 8, pltpu.roll(east, LANES - 8 * group, 1) if group else east, moved
                )

    def row_halo(side):
        mine = pl.ds(PAD if side == 0 else PAD + rows_all - 8, 8)
        theirs = pl.ds(PAD + rows_all if side == 0 else PAD - 8, 8)
        return remote(
            E.at[:, mine, mid], E.at[:, theirs, mid], row_send.at[side], row_recv.at[side], (north, south)[side]
        )

    @pl.loop(0, chunks + 2)
    def _(i):
        @pl.when(i < chunks)
        def _():
            column_pass(order(i))

        @pl.when(i == 0)
        def _():
            pl.semaphore_wait(barrier, 3 + (strip + strips - 1) // strips + (2 * strips - 2 - strip) // strips)

            pl.when(has_down)(lambda: down_p().start())

            @pl.loop(0, early)
            def _(e):
                pl.when(has_up)(lambda: up_message(0, e).start())

        @pl.when(i == chunks)
        def _():
            for copy in small:
                copy.wait()

        @pl.when(i >= chunks)
        def _():
            finish(order(i - chunks))

        @pl.when(i > 1)
        def _():
            chunk = order(i - 2)
            stage1(chunk).wait_recv()
            xs[chunk] = part[chunk, core, 1 - chip] + recv1[chunk, 1 - chip]

        @pl.when(i < chunks)
        def _():
            stage1(order(i)).start()

        @pl.when(i > 1)
        def _():
            stage2(order(i - 2)).start()

    def post_faces(first, last_one):
        @pl.loop(first, last_one)
        def _(e):
            @pl.when(has_up)
            def _():
                pl.when(e >= early)(lambda: up_message(0, e).start())
                up_message(1, e).start()

    @pl.when(depth == 0)
    def _():
        moist[0] = moist[0] + face_scale * rain[...]

    def face_step(e):
        where = pl.ds(pl.multiple_of(e * RE, RE), RE)

        @pl.when(has_down)
        def _():
            remote(up_pc.at[e], up_pc.at[e], face_send.at[2], up_recv.at[e], below).wait_recv()
            value = flux(pbuf[last, where, part_b], c7[where, part_b], up_pc[e, 0], up_pc[e, 1])
            fb_out[where] = value
            moist[last, where, part_b] = moist[last, where, part_b] - value
            flux_down(e).start()

        @pl.when(has_up)
        def _():
            @pl.when(e == 0)
            def _():
                down_p().wait_recv()
                down_c(0).wait_recv()

            pl.when(e == edges // 2)(lambda: down_c(1).wait_recv())
            value = flux(dn_p[where], dn_c[where], pbuf[0, where, part_a], c0[where, part_a])
            fa_out[where] = value
            moist[0, where, part_a] = moist[0, where, part_a] + value
            flux_up(e).start()

    sub = lax.broadcasted_iota(jnp.int32, (8, wide), 0)

    def rows_of(t, count=1):
        return pl.ds(pl.multiple_of(8 * t, 8), 8 * count)

    def around(ref, q, t):
        north_t, a, b, south_t = (ref[q, rows_of(t + k), :] for k in (-1, 0, 1, 2))

        def sums(before, here, after):
            down = [pltpu.roll(v, 1, 0) for v in (before, here)]
            up = [pltpu.roll(v, 7, 0) for v in (here, after)]
            return (
                pltpu.roll(here, 1, 1)
                + pltpu.roll(here, wide - 1, 1)
                + jnp.where(sub == 0, down[0], down[1])
                + jnp.where(sub == 7, up[1], up[0])
            )

        return jnp.concatenate([sums(north_t, a, b), sums(a, b, south_t)], axis=0)

    def wave(j, stages):
        at = (2 * j + 2, 2 * j, 2 * j - 3, 2 * j - 6)
        out = []
        if 3 in stages:
            here = rows_of(at[3], 2)
            out.append((H, 2, here, A[2, here, :] + A[3, here, :] * around(H, 1, at[3])))
        if 2 in stages:
            here = rows_of(at[2], 2)
            out.append((H, 1, here, A[0, here, :] + A[1, here, :] * around(H, 0, at[2])))
        if 1 in stages:
            here = rows_of(at[1], 2)
            out.append((H, 0, here, A[0, here, :] + A[1, here, :] * around(E, 3, at[1])))
        if 0 in stages:
            here = rows_of(at[0], 2)
            root = E[0, here, :]
            scale = 1.0 / (E[1, here, :] + root * around(E, 0, at[0]))
            free, bound = E[2, here, :] * scale, root * scale
            out += [(A, 0, here, root * free), (A, 1, here, root * bound), (A, 2, here, free), (A, 3, here, bound)]
        for ref, q, here, value in out:
            ref[q, here, :] = value

    def head_copy(chunk, source):
        where = pl.ds(pl.multiple_of(chunk * R, R), R)
        return remote(
            heads.at[source, where], heads.at[source, where],
            head_send.at[0], head_recv.at[source], {"depth": 3},
        )

    def hand_on(chunk):
        where = pl.ds(pl.multiple_of(chunk * R, R), R)
        value = H[SWEEPS - 1, pl.ds(pl.multiple_of(PAD + chunk * R, 8), R), mid]
        heads[depth, where] = value
        head[where, :] = value
        pl.when(depth < 3)(lambda: head_copy(chunk, depth).start())

    pl.when(has_north)(lambda: row_halo(0).start())
    pl.when(has_south)(lambda: row_halo(1).start())

    @pl.loop(1, chunks - 3)
    def _(chunk):
        finish(chunk)

    pl.when(has_down)(lambda: down_c(0).start())
    post_faces(0, 1)
    finish(chunks - 3)
    post_faces(1, 2)
    finish(chunks - 2)
    pl.when(has_down)(lambda: down_c(1).start())

    pl.when(has_south)(lambda: row_halo(0).wait_recv())
    pl.when(has_north)(lambda: row_halo(1).wait_recv())
    pack(chunks, halo_tiles)
    post_faces(2, edges)

    @pl.loop(0, chunks - 3)
    def _(chunk):
        unpack(chunk)

    unpack(chunks - 1)
    unpack(chunks, halo_tiles)

    every = (0, 1, 2, 3)
    wave(0, (0,))
    wave(1, (0, 1))
    wave(2, (0, 1, 2))
    wave(3, (0, 1, 2))
    wave(4, (0, 1, 2, 3))
    face_step(0)

    @pl.loop(5, chunks - 1)
    def _(j):
        unpack(j)
        wave(j, every)
        hand_on(j - 5)

    face_step(1)

    @pl.loop(chunks - 1, chunks + 1)
    def _(j):
        wave(j, every)
        hand_on(j - 5)

    for j, stages in ((chunks + 1, (1, 2, 3)), (chunks + 2, (2, 3)), (chunks + 3, (2, 3)), (chunks + 4, (3,))):
        wave(j, stages)
        hand_on(j - 5)

    @pl.loop(2, edges)
    def _(e):
        face_step(e)

    @pl.when(depth == 3)
    def _():
        for block in range(4):
            if block < 3:
                remote(heads.at[block], heads.at[block], head_send.at[0], head_recv.at[block], {"depth": 0}).wait_recv()
            cols = pl.ds(block * tile, tile)
            bottom = c7[:, cols] * (
                (pbuf[last, :, cols] - heads[block]) * (2.0 * face_scale / layer_thick) + face_scale
            )
            moist[last, :, cols] = moist[last, :, cols] - bottom

    @pl.when(has_down)
    def _():
        remote(fa_in, fa_in, face_send.at[5], fa_recv.at[0], below).wait_recv()
        moist[last, :, part_a] = moist[last, :, part_a] - fa_in[...]

    @pl.when(has_up)
    def _():
        @pl.loop(0, edges)
        def _(e):
            where = pl.ds(pl.multiple_of(e * RE, RE), RE)
            flux_down(e).wait_recv()
            moist[0, where, part_b] = moist[0, where, part_b] + fb_in[where]

    remote(part.at[:, 1 - core], recv1, s1_send.at[0], s1_recv.at[0], mate).wait_send()
    remote(xs, recv2, s2_send.at[0], s2_recv.at[0], cross).wait_send()

    @pl.when(has_down)
    def _():
        down_p().wait_send()
        remote(c7.at[:, part_a], dn_c, face_send.at[1], down_recv.at[1], below).wait_send()
        remote(fb_out, fb_in, face_send.at[4], fb_recv.at[0], below).wait_send()
        remote(colsend.at[0], colrecv.at[0], col_send.at[0], col_recv.at[0, 0], below).wait_send()
        remote(heads.at[depth], heads.at[depth], head_send.at[0], head_recv.at[depth], {"depth": 3}).wait_send()

    @pl.when(has_up)
    def _():
        remote(p_hbm.at[0, :, part_b], fb_in, face_send.at[2], up_recv.at[0], above).wait_send()
        remote(c0.at[:, part_b], fb_in, face_send.at[3], up_recv.at[0], above).wait_send()
        remote(fa_out, fa_in, face_send.at[5], fa_recv.at[0], above).wait_send()
        remote(colsend.at[1], colrecv.at[1], col_send.at[1], col_recv.at[1, 0], above).wait_send()

    pl.when(has_north)(lambda: row_halo(0).wait_send())
    pl.when(has_south)(lambda: row_halo(1).wait_send())


def store_kernel(moist, head, moist_out, head_out, sems):
    copies = [pltpu.make_async_copy(head, head_out, sems.at[0])]
    for k in range(moist.shape[0]):
        copies.append(pltpu.make_async_copy(moist.at[k], moist_out.at[k], sems.at[k + 1]))
    for copy in copies:
        copy.start()
    for copy in copies:
        copy.wait()


def shards(strips, pressure, texture, active, rain, k_sat, alpha, theta_sat, head_old, cell_code, section):
    layers, rows, cols = pressure.shape
    tile = head_old.shape[1]
    wide = tile + LANES
    cols_a = 3 * LANES
    cols_b = cols - cols_a
    chunks, edges = rows // R, rows // RE
    f32 = jnp.float32
    vmem = lambda *shape: pltpu.VMEM(shape, f32)
    dma = lambda *shape: pltpu.SemaphoreType.DMA(shape)
    table = pltpu.SMEM(k_sat.shape, f32)
    scratch = [
        table,
        table,
        table,
        vmem(layers, rows, cols),
        pltpu.VMEM((layers, rows, cols), jnp.int32),
        pltpu.VMEM((layers, rows, cols), jnp.int32),
        vmem(rows, cols),
        vmem(rows, tile),
        pltpu.VMEM((rows, tile), jnp.int32),
        vmem(rows, tile),
        vmem(3, 2, 8, LANES),
        vmem(chunks, 2, 2, 3, R, tile),
        vmem(chunks, 2, 3, R, tile),
        vmem(chunks, 3, R, tile),
        vmem(chunks, 3, R, tile),
        vmem(rows, cols),
        vmem(rows, cols),
        vmem(rows, cols_a),
        vmem(rows, cols_a),
        vmem(edges, 2, RE, cols_b),
        vmem(rows, cols_b),
        vmem(rows, cols_b),
        vmem(rows, cols_a),
        vmem(rows, cols_a),
        vmem(4, rows + 2 * PAD, wide),
        vmem(SWEEPS, rows + 2 * PAD, wide),
        vmem(4, rows + 2 * PAD, wide),
        vmem(2, chunks + 1, 8, LANES),
        vmem(2, chunks + 1, 8, LANES),
        vmem(4, rows, tile),
        dma(3, chunks),
        dma(7),
        dma(1),
        dma(chunks),
        dma(1),
        dma(chunks),
        dma(6),
        dma(3),
        dma(edges),
        dma(edges),
        dma(1),
        dma(2),
        dma(2, chunks + 1),
        dma(2),
        dma(2),
        dma(1),
        dma(4),
    ]
    anywhere = pl.BlockSpec(memory_space=pltpu.HBM)
    moist, head = pl.pallas_call(
        functools.partial(kernel, strips),
        out_shape=(
            pltpu.VMEM((layers, rows, cols), f32),
            pltpu.VMEM((rows, tile), f32),
        ),
        in_specs=[anywhere] * 10,
        out_specs=(pl.BlockSpec(memory_space=pltpu.VMEM), pl.BlockSpec(memory_space=pltpu.VMEM)),
        scratch_shapes=scratch,
        compiler_params=pltpu.CompilerParams(
            collective_id=0, has_side_effects=True, vmem_limit_bytes=59 * 2**20
        ),
        name="soil_column",
    )(k_sat, alpha, theta_sat, pressure, texture, active, rain, head_old, cell_code, section)
    on_chip = pl.BlockSpec(memory_space=pltpu.VMEM)
    return pl.pallas_call(
        store_kernel,
        out_shape=(
            jax.ShapeDtypeStruct((layers, rows, cols), f32),
            jax.ShapeDtypeStruct((rows, tile), f32),
        ),
        in_specs=[on_chip] * 2,
        out_specs=(anywhere, anywhere),
        scratch_shapes=[dma(layers + 1)],
        compiler_params=pltpu.CompilerParams(vmem_limit_bytes=2**20),
        name="store",
    )(pltpu.with_memory_space_constraint(moist, pltpu.VMEM), pltpu.with_memory_space_constraint(head, pltpu.VMEM))


def solution(mesh):
    in_specs = (
        P("depth", "strips", None),
        P("depth", "strips", None),
        P("depth", "strips", None),
        P("strips", None),
        P(),
        P(),
        P(),
        P("strips", "depth"),
        P("strips", "depth"),
        P("strips", "depth"),
    )
    out_specs = (P("depth", "strips", None), P("strips", "depth"))
    body = functools.partial(shards, mesh.shape["strips"])
    return jax.shard_map(body, mesh=mesh, in_specs=in_specs, out_specs=out_specs, check_vma=False)
```

time: 37.6 us -> 32.7 us (0.87)
  the two profiles are of different devices: /device:TPU:104 before, /device:TPU:97 now
where the time goes in v3:
time: 32.7 us; the launch traced here: 32.6 us
  Pallas kernels  32 us (98%)
  between operations  0.64 us (2%)
    pallas_call x1, Pallas kernels, shards(): pl.pallas_call(functools.partial(kernel, strips), out_shape=(pltpu.VMEM((...  29.8 us
    pallas_call x1, Pallas kernels, shards(): pl.pallas_call(store_kernel, out_shape=(jax.ShapeDtypeStruct((layers, row...  2.12 us

profile of v3, /device:TPU:97, one launch (start us, length us, event | category | flops | bytes accessed | tf_op | source)
XLA Modules:
  0.0 32.6 jit_solution(9813247649705190417)
XLA Ops:
  0.6 29.8 %soil_column.1 = (f32[8,128,1024]{2,1,0:T(8,128)S(1)}, f32[128,256]{1,0:T(8,128)S(1)}) custom-call(f32[12]{0:T(128)} %ks_hbm.1, f32[12]{0:T(128)} %al_hbm.1, f32[12]{0:T(128)} %th_hbm.1, f32[8,128,1024]{2,1,0:T(8,128)} %p_hbm.1, s32[8,128,1024]{2,1,0:T(8,128)} %t_hbm.1, s32[8,128,1024]{2,1,0:T(8,128)} %a_hbm.1, f32[128,1024]{1,0:T(8,128)} %rain_hbm.1, ...), custom_call_target="tpu_custom_call" | custom-call | tf_op jit(solution)/shard_map/soil_column/pallas_call | solution.py:595
  30.5 2.1 %store.1 = (f32[8,128,1024]{2,1,0:T(8,128)}, f32[128,256]{1,0:T(8,128)}) custom-call(f32[8,128,1024]{2,1,0:T(8,128)S(1)} %get-tuple-element.4.moist, f32[128,256]{1,0:T(8,128)S(1)} %get-tuple-element.5.head), custom_call_target="tpu_custom_call" | custom-call | tf_op jit(solution)/shard_map/store/pallas_call | solution.py:610

commit v4 on v3

--- a/solution.py
+++ b/solution.py
@@ -21,6 +21,7 @@
 
 R = 16
 RE = R
+XS, YS = 4, 2
 PAD = 24
 LANES = 128
 
@@ -59,7 +60,7 @@
     dn_p, dn_c, up_pc, fb_out, fb_in, fa_out, fa_in,
     E, H, A, colsend, colrecv, heads,
     load_sem, misc_sem, s1_send, s1_recv, s2_send, s2_recv,
-    face_send, down_recv, up_recv, fb_recv, fa_recv, col_send, col_recv, row_send, row_recv, head_send, head_recv,
+    face_send, down_recv, up_recv, fb_recv, fa_recv, col_send, col_recv, row_send, row_recv, head_send, head_recv, known,
 ):
     layers, rows_all, cols_all = pbuf.shape
     chunks, edges = rows_all // R, rows_all // RE
@@ -91,10 +92,42 @@
     def greet(device):
         pl.semaphore_signal(barrier, inc=1, device_id=device, device_id_type=MESH)
 
+    x, y, z, z_count = strip % XS, strip // XS % YS, strip // (XS * YS), strips // (XS * YS)
+    start, end = x == 0, x == XS - 1
+    corner = start & (y == 0)
     for step in (1, 2, 3):
         greet({"depth": (depth + step) % 4})
-    pl.when(has_north)(lambda: greet(north))
-    pl.when(has_south)(lambda: greet(south))
+    greet({"strips": strip - x + (x + 1) % XS})
+    greet({"strips": strip - x + (x + XS - 1) % XS})
+    pl.when(start)(lambda: greet({"strips": strip + XS - 2 * XS * y}))
+    pl.when(corner & (z > 0))(lambda: greet({"strips": strip - XS * YS}))
+    pl.when(corner & (z < z_count - 1))(lambda: greet({"strips": strip + XS * YS}))
+    is_start = (XS - x) // XS
+    z_sides = (z + z_count - 1) // z_count + (2 * z_count - 2 - z) // z_count
+    greeted = 5 + is_start + is_start * (1 - y) * z_sides
+
+    def announce(which, target):
+        pl.semaphore_signal(known.at[which], inc=1, device_id={"strips": target}, device_id_type=MESH)
+
+    def announce_first():
+        @pl.when(corner)
+        def _():
+            announce(0, strip + XS - 1)
+            announce(0, strip + XS)
+            pl.when(z < z_count - 1)(lambda: announce(1, strip + XS))
+
+        pl.when(start & (y == 1) & (z < z_count - 1))(lambda: announce(1, strip - XS))
+
+    def announce_second():
+        @pl.when(start & (z < z_count - 1))
+        def _():
+            pl.semaphore_wait(known.at[1], 1)
+            pl.when(y == 0)(lambda: announce(2, strip + XS * YS))
+            pl.when(y == 1)(lambda: announce(2, strip + XS - 1))
+
+    def await_announced():
+        pl.when((end & (y == 0)) | (start & (y == 1)))(lambda: pl.semaphore_wait(known.at[0], 1))
+        pl.when((end & (y == 1) & has_south) | (corner & has_north))(lambda: pl.semaphore_wait(known.at[2], 1))
 
     def load(which, chunk):
         src, dst = ((p_hbm, pbuf), (t_hbm, tbuf), (a_hbm, abuf))[which]
@@ -204,12 +237,13 @@
 
     half = rows_all // 2
 
-    def down_p():
-        return remote(p_hbm.at[last, :, part_a], dn_p, face_send.at[0], down_recv.at[0], below)
+    def down_p(k):
+        where = pl.ds(k * half, half)
+        return remote(p_hbm.at[last, where, part_a], dn_p.at[where], face_send.at[0], down_recv.at[2 + k], below)
 
     def down_c(k):
         where = pl.ds(k * half, half)
-        return remote(c7.at[where, part_a], dn_c.at[where], face_send.at[1], down_recv.at[1 + k], below)
+        return remote(c7.at[where, part_a], dn_c.at[where], face_send.at[1], down_recv.at[k], below)
 
     def up_message(which, e):
         where = pl.ds(pl.multiple_of(e * RE, RE), RE)
@@ -298,13 +332,16 @@
 
         @pl.when(i == 0)
         def _():
-            pl.semaphore_wait(barrier, 3 + (strip + strips - 1) // strips + (2 * strips - 2 - strip) // strips)
-
-            pl.when(has_down)(lambda: down_p().start())
+            pl.semaphore_wait(barrier, greeted)
+            announce_first()
+
+            pl.when(has_down)(lambda: down_p(0).start())
 
             @pl.loop(0, early)
             def _(e):
                 pl.when(has_up)(lambda: up_message(0, e).start())
+
+        pl.when(i == chunks // 2)(announce_second)
 
         @pl.when(i == chunks)
         def _():
@@ -354,12 +391,13 @@
 
         @pl.when(has_up)
         def _():
-            @pl.when(e == 0)
-            def _():
-                down_p().wait_recv()
-                down_c(0).wait_recv()
-
-            pl.when(e == edges // 2)(lambda: down_c(1).wait_recv())
+            for k in range(2):
+
+                @pl.when(e == k * (edges // 2))
+                def _():
+                    down_p(k).wait_recv()
+                    down_c(k).wait_recv()
+
             value = flux(dn_p[where], dn_c[where], pbuf[0, where, part_a], c0[where, part_a])
             fa_out[where] = value
             moist[0, where, part_a] = moist[0, where, part_a] + value
@@ -420,30 +458,38 @@
         head[where, :] = value
         pl.when(depth < 3)(lambda: head_copy(chunk, depth).start())
 
+    await_announced()
     pl.when(has_north)(lambda: row_halo(0).start())
     pl.when(has_south)(lambda: row_halo(1).start())
 
-    @pl.loop(1, chunks - 3)
-    def _(chunk):
-        finish(chunk)
-
-    pl.when(has_down)(lambda: down_c(0).start())
-    post_faces(0, 1)
-    finish(chunks - 3)
-    post_faces(1, 2)
-    finish(chunks - 2)
-    pl.when(has_down)(lambda: down_c(1).start())
+    def posts(down, up):
+        if down is not None:
+            pl.when(has_down)(lambda: down.start())
+        post_faces(*up)
+
+    finish(1)
+    finish(2)
+    finish(3)
+    posts(down_c(0), (0, 2))
+    finish(4)
+    posts(None, (2, 3))
+    finish(5)
+    posts(down_c(1), (3, 4))
+    finish(6)
 
     pl.when(has_south)(lambda: row_halo(0).wait_recv())
     pl.when(has_north)(lambda: row_halo(1).wait_recv())
     pack(chunks, halo_tiles)
-    post_faces(2, edges)
+    posts(down_p(1), (4, edges))
+    face_step(0)
+    face_step(1)
 
     @pl.loop(0, chunks - 3)
     def _(chunk):
         unpack(chunk)
 
     unpack(chunks - 1)
+    face_step(2)
     unpack(chunks, halo_tiles)
 
     every = (0, 1, 2, 3)
@@ -452,7 +498,7 @@
     wave(2, (0, 1, 2))
     wave(3, (0, 1, 2))
     wave(4, (0, 1, 2, 3))
-    face_step(0)
+    face_step(3)
 
     @pl.loop(5, chunks - 1)
     def _(j):
@@ -460,7 +506,7 @@
         wave(j, every)
         hand_on(j - 5)
 
-    face_step(1)
+    face_step(4)
 
     @pl.loop(chunks - 1, chunks + 1)
     def _(j):
@@ -471,7 +517,7 @@
         wave(j, stages)
         hand_on(j - 5)
 
-    @pl.loop(2, edges)
+    @pl.loop(5, edges)
     def _(e):
         face_step(e)
 
@@ -504,7 +550,7 @@
 
     @pl.when(has_down)
     def _():
-        down_p().wait_send()
+        remote(p_hbm.at[last, :, part_a], dn_p, face_send.at[0], down_recv.at[2], below).wait_send()
         remote(c7.at[:, part_a], dn_c, face_send.at[1], down_recv.at[1], below).wait_send()
         remote(fb_out, fb_in, face_send.at[4], fb_recv.at[0], below).wait_send()
         remote(colsend.at[0], colrecv.at[0], col_send.at[0], col_recv.at[0, 0], below).wait_send()
@@ -580,7 +626,7 @@
         dma(1),
         dma(chunks),
         dma(6),
-        dma(3),
+        dma(4),
         dma(edges),
         dma(edges),
         dma(1),
@@ -590,6 +636,7 @@
         dma(2),
         dma(1),
         dma(4),
+        pltpu.SemaphoreType.REGULAR((3,)),
     ]
     anywhere = pl.BlockSpec(memory_space=pltpu.HBM)
     moist, head = pl.pallas_call(

time: 32.7 us -> 29.8 us (0.911)
  the two profiles are of different devices: /device:TPU:97 before, /device:TPU:1 now
where the time goes in v4:
time: 29.8 us; the launch traced here: 29.7 us
  Pallas kernels  29.1 us (98%)
  between operations  0.64 us (2%)
    pallas_call x1, Pallas kernels, shards(): pl.pallas_call(functools.partial(kernel, strips), out_shape=(pltpu.VMEM((...  26.9 us
    pallas_call x1, Pallas kernels, shards(): pl.pallas_call(store_kernel, out_shape=(jax.ShapeDtypeStruct((layers, row...  2.12 us

profile of v4, /device:TPU:1, one launch (start us, length us, event | category | flops | bytes accessed | tf_op | source)
XLA Modules:
  0.0 29.7 jit_solution(9202532976947281773)
XLA Ops:
  0.6 26.9 %soil_column.1 = (f32[8,128,1024]{2,1,0:T(8,128)S(1)}, f32[128,256]{1,0:T(8,128)S(1)}) custom-call(f32[12]{0:T(128)} %ks_hbm.1, f32[12]{0:T(128)} %al_hbm.1, f32[12]{0:T(128)} %th_hbm.1, f32[8,128,1024]{2,1,0:T(8,128)} %p_hbm.1, s32[8,128,1024]{2,1,0:T(8,128)} %t_hbm.1, s32[8,128,1024]{2,1,0:T(8,128)} %a_hbm.1, f32[128,1024]{1,0:T(8,128)} %rain_hbm.1, ...), custom_call_target="tpu_custom_call" | custom-call | tf_op jit(solution)/shard_map/soil_column/pallas_call | solution.py:642
  27.6 2.1 %store.1 = (f32[8,128,1024]{2,1,0:T(8,128)}, f32[128,256]{1,0:T(8,128)}) custom-call(f32[8,128,1024]{2,1,0:T(8,128)S(1)} %get-tuple-element.4.moist, f32[128,256]{1,0:T(8,128)S(1)} %get-tuple-element.5.head), custom_call_target="tpu_custom_call" | custom-call | tf_op jit(solution)/shard_map/store/pallas_call | solution.py:657

commit v5 on v4

--- a/solution.py
+++ b/solution.py
@@ -21,6 +21,7 @@
 
 R = 16
 RE = R
+EARLY = 4
 XS, YS = 4, 2
 PAD = 24
 LANES = 128
@@ -58,7 +59,7 @@
     moist, head,
     ks, al, th, pbuf, tbuf, abuf, rain, h0, code, sec, tabs, part, recv1, xs, recv2, c0, c7,
     dn_p, dn_c, up_pc, fb_out, fb_in, fa_out, fa_in,
-    E, H, A, colsend, colrecv, heads,
+    E, H, A, colsend, colrecv, heads, rowsend, rowrecv,
     load_sem, misc_sem, s1_send, s1_recv, s2_send, s2_recv,
     face_send, down_recv, up_recv, fb_recv, fa_recv, col_send, col_recv, row_send, row_recv, head_send, head_recv, known,
 ):
@@ -77,7 +78,6 @@
     cross = {"depth": (depth + 2) % 4}
     above, below = {"depth": depth - 1}, {"depth": depth + 1}
     north, south = {"strips": strip - 1}, {"strips": strip + 1}
-    early = edges // 3
     has_up, has_down = depth > 0, depth < 3
     has_north, has_south = strip > 0, strip < strips - 1
 
@@ -132,14 +132,14 @@
     def load(which, chunk):
         src, dst = ((p_hbm, pbuf), (t_hbm, tbuf), (a_hbm, abuf))[which]
         where = pl.ds(pl.multiple_of(chunk * R, R), R)
-        return pltpu.make_async_copy(src.at[:, where, :], dst.at[:, where, :], load_sem.at[which, chunk])
+        return pltpu.make_async_copy(src.at[:, where, :], dst.at[:, where, :], load_sem.at[chunk])
 
     small = [
-        pltpu.make_async_copy(src, dst, misc_sem.at[i])
+        pltpu.make_async_copy(src, dst, misc_sem.at[0])
         for i, (src, dst) in enumerate(((h_hbm, h0), (code_hbm, code), (sec_hbm, sec), (rain_hbm, rain)))
     ]
     tables = [
-        pltpu.make_async_copy(src, dst, misc_sem.at[4 + i])
+        pltpu.make_async_copy(src, dst, misc_sem.at[1 + i])
         for i, (src, dst) in enumerate(((ks_hbm, ks), (al_hbm, al), (th_hbm, th)))
     ]
     for copy in tables:
@@ -198,8 +198,6 @@
         return remote(xs.at[chunk], recv2.at[chunk], s2_send.at[0], s2_recv.at[chunk], cross)
 
     def column_pass(chunk):
-        for which in range(3):
-            load(which, chunk).wait()
         where = pl.ds(pl.multiple_of(chunk * R, R), R)
 
         def lane_tile(block, half):
@@ -237,9 +235,10 @@
 
     half = rows_all // 2
 
-    def down_p(k):
-        where = pl.ds(k * half, half)
-        return remote(p_hbm.at[last, where, part_a], dn_p.at[where], face_send.at[0], down_recv.at[2 + k], below)
+    def down_p(e):
+        where = pl.ds(pl.multiple_of(e * RE, RE), RE)
+        k = e // (edges // 2)
+        return remote(pbuf.at[last, where, part_a], dn_p.at[where], face_send.at[0], down_recv.at[2 + k], below)
 
     def down_c(k):
         where = pl.ds(k * half, half)
@@ -247,12 +246,12 @@
 
     def up_message(which, e):
         where = pl.ds(pl.multiple_of(e * RE, RE), RE)
-        src = p_hbm.at[0, where, part_b] if which == 0 else c0.at[where, part_b]
+        src = (pbuf.at[0, where, part_b], c0.at[where, part_b])[which]
         return remote(src, up_pc.at[e, which], face_send.at[2 + which], up_recv.at[e], above)
 
     def flux_down(e):
         where = pl.ds(pl.multiple_of(e * RE, RE), RE)
-        return remote(fb_out.at[where], fb_in.at[where], face_send.at[4], fb_recv.at[e], below)
+        return remote(fb_out.at[where], fb_in.at[where], face_send.at[4], fb_recv.at[0], below)
 
     def flux_up(e):
         where = pl.ds(pl.multiple_of(e * RE, RE), RE)
@@ -281,7 +280,7 @@
     def column_halo(side, chunk):
         return remote(
             colsend.at[side, chunk], colrecv.at[side, chunk],
-            col_send.at[side], col_recv.at[side, chunk], (below, above)[side],
+            col_send.at[side], col_recv.at[chunk], (below, above)[side],
         )
 
     def pack_tiles(side, chunk, tiles):
@@ -306,8 +305,15 @@
         pl.when(has_up)(lambda: pack_tiles(1, chunk, tiles))
 
     def unpack(chunk, tiles=None):
-        pl.when(has_up)(lambda: column_halo(0, chunk).wait_recv())
-        pl.when(has_down)(lambda: column_halo(1, chunk).wait_recv())
+        pl.when(depth == 0)(lambda: column_halo(1, chunk).wait_recv())
+        pl.when(depth == 3)(lambda: column_halo(0, chunk).wait_recv())
+
+        @pl.when(has_up & has_down)
+        def _():
+            remote(
+                colsend.at[:, chunk], colrecv.at[:, chunk], col_send.at[0], col_recv.at[chunk], below
+            ).wait_recv()
+
         west, east = colrecv[0, chunk], colrecv[1, chunk]
         for q in range(4):
             for h in range(2):
@@ -317,36 +323,62 @@
                     lane < 8, pltpu.roll(east, LANES - 8 * group, 1) if group else east, moved
                 )
 
+    row8 = lax.broadcasted_iota(jnp.int32, (8, LANES), 0)
+    turns = ((0, 3, 6, 0, 2), (3, 6, 0, 2, 4))
+
+    def turned(value, shift):
+        return pltpu.roll(value, shift % 8, 0) if shift % 8 else value
+
     def row_halo(side):
+        return remote(rowsend.at[side], rowrecv.at[side], row_send.at[side], row_recv.at[side], (north, south)[side])
+
+    def send_rows(side):
         mine = pl.ds(PAD if side == 0 else PAD + rows_all - 8, 8)
+        for k in range(2):
+            cols = pl.ds(k * LANES, LANES)
+            root, product, base = (turned(E[q, mine, cols], turns[side][n]) for n, q in enumerate((0, 3, 1)))
+            rowsend[side, :, cols] = jnp.where(row8 < 3, root, jnp.where(row8 < 6, product, base))
+        first, second = (turned(E[2, mine, pl.ds(k * LANES, LANES)], turns[side][3 + k]) for k in range(2))
+        rowsend[side, :, 2 * LANES :] = jnp.where(row8 < 2, first, second)
+        row_halo(side).start()
+
+    def take_rows(side):
+        row_halo(side).wait_recv()
         theirs = pl.ds(PAD + rows_all if side == 0 else PAD - 8, 8)
-        return remote(
-            E.at[:, mine, mid], E.at[:, theirs, mid], row_send.at[side], row_recv.at[side], (north, south)[side]
-        )
+        for k in range(2):
+            cols = pl.ds(k * LANES, LANES)
+            value = rowrecv[side, :, cols]
+            for n, q in enumerate((0, 3, 1)):
+                E[q, theirs, cols] = turned(value, 8 - turns[side][n])
+            E[2, theirs, cols] = turned(rowrecv[side, :, 2 * LANES :], 8 - turns[side][3 + k])
 
     @pl.loop(0, chunks + 2)
     def _(i):
         @pl.when(i < chunks)
         def _():
-            column_pass(order(i))
+            three = pl.ds(0, 3 * R)
+            pltpu.make_async_copy(p_hbm.at[:, three, :], pbuf.at[:, three, :], load_sem.at[order(i)]).wait()
 
         @pl.when(i == 0)
         def _():
             pl.semaphore_wait(barrier, greeted)
             announce_first()
 
-            pl.when(has_down)(lambda: down_p(0).start())
-
-            @pl.loop(0, early)
-            def _(e):
-                pl.when(has_up)(lambda: up_message(0, e).start())
+        @pl.when(i < EARLY)
+        def _():
+            pl.when(has_down)(lambda: down_p(order(i)).start())
+            pl.when(has_up)(lambda: up_message(0, order(i)).start())
+
+        @pl.when(i < chunks)
+        def _():
+            column_pass(order(i))
 
         pl.when(i == chunks // 2)(announce_second)
 
         @pl.when(i == chunks)
         def _():
-            for copy in small:
-                copy.wait()
+            seven = pl.ds(0, 3 + cols_all // tile)
+            pltpu.make_async_copy(p_hbm.at[seven, :, mid], pbuf.at[seven, :, mid], misc_sem.at[0]).wait()
 
         @pl.when(i >= chunks)
         def _():
@@ -371,7 +403,7 @@
         def _(e):
             @pl.when(has_up)
             def _():
-                pl.when(e >= early)(lambda: up_message(0, e).start())
+                pl.when((e >= EARLY - 1) & (e < edges - 1))(lambda: up_message(0, e).start())
                 up_message(1, e).start()
 
     @pl.when(depth == 0)
@@ -395,7 +427,8 @@
 
                 @pl.when(e == k * (edges // 2))
                 def _():
-                    down_p(k).wait_recv()
+                    where = pl.ds(k * half, half)
+                    remote(dn_p.at[where], dn_p.at[where], face_send.at[0], down_recv.at[2 + k], above).wait_recv()
                     down_c(k).wait_recv()
 
             value = flux(dn_p[where], dn_c[where], pbuf[0, where, part_a], c0[where, part_a])
@@ -459,28 +492,28 @@
         pl.when(depth < 3)(lambda: head_copy(chunk, depth).start())
 
     await_announced()
-    pl.when(has_north)(lambda: row_halo(0).start())
-    pl.when(has_south)(lambda: row_halo(1).start())
+    pl.when(has_north)(lambda: send_rows(0))
+    pl.when(has_south)(lambda: send_rows(1))
 
     def posts(down, up):
-        if down is not None:
-            pl.when(has_down)(lambda: down.start())
+        for copy in down:
+            pl.when(has_down)(copy)
         post_faces(*up)
 
     finish(1)
     finish(2)
     finish(3)
-    posts(down_c(0), (0, 2))
+    posts([lambda: down_c(0).start()], (0, 2))
     finish(4)
-    posts(None, (2, 3))
+    posts([lambda: down_p(EARLY - 1).start()], (2, 3))
     finish(5)
-    posts(down_c(1), (3, 4))
+    posts([lambda: down_c(1).start()], (3, 4))
     finish(6)
 
-    pl.when(has_south)(lambda: row_halo(0).wait_recv())
-    pl.when(has_north)(lambda: row_halo(1).wait_recv())
+    pl.when(has_south)(lambda: take_rows(0))
+    pl.when(has_north)(lambda: take_rows(1))
     pack(chunks, halo_tiles)
-    posts(down_p(1), (4, edges))
+    posts([lambda e=e: down_p(e).start() for e in range(EARLY, edges - 1)], (4, edges))
     face_step(0)
     face_step(1)
 
@@ -539,29 +572,26 @@
 
     @pl.when(has_up)
     def _():
-        @pl.loop(0, edges)
-        def _(e):
-            where = pl.ds(pl.multiple_of(e * RE, RE), RE)
-            flux_down(e).wait_recv()
-            moist[0, where, part_b] = moist[0, where, part_b] + fb_in[where]
+        remote(fb_in, fb_in, face_send.at[4], fb_recv.at[0], above).wait_recv()
+        moist[0, :, part_b] = moist[0, :, part_b] + fb_in[...]
 
     remote(part.at[:, 1 - core], recv1, s1_send.at[0], s1_recv.at[0], mate).wait_send()
     remote(xs, recv2, s2_send.at[0], s2_recv.at[0], cross).wait_send()
 
     @pl.when(has_down)
     def _():
-        remote(p_hbm.at[last, :, part_a], dn_p, face_send.at[0], down_recv.at[2], below).wait_send()
+        remote(c7.at[:, part_a], dn_p, face_send.at[0], down_recv.at[2], below).wait_send()
         remote(c7.at[:, part_a], dn_c, face_send.at[1], down_recv.at[1], below).wait_send()
         remote(fb_out, fb_in, face_send.at[4], fb_recv.at[0], below).wait_send()
-        remote(colsend.at[0], colrecv.at[0], col_send.at[0], col_recv.at[0, 0], below).wait_send()
+        remote(colsend.at[0], colrecv.at[0], col_send.at[0], col_recv.at[0], below).wait_send()
         remote(heads.at[depth], heads.at[depth], head_send.at[0], head_recv.at[depth], {"depth": 3}).wait_send()
 
     @pl.when(has_up)
     def _():
-        remote(p_hbm.at[0, :, part_b], fb_in, face_send.at[2], up_recv.at[0], above).wait_send()
+        remote(c0.at[:, part_b], fb_in, face_send.at[2], up_recv.at[0], above).wait_send()
         remote(c0.at[:, part_b], fb_in, face_send.at[3], up_recv.at[0], above).wait_send()
         remote(fa_out, fa_in, face_send.at[5], fa_recv.at[0], above).wait_send()
-        remote(colsend.at[1], colrecv.at[1], col_send.at[1], col_recv.at[1, 0], above).wait_send()
+        remote(colsend.at[1], colrecv.at[1], col_send.at[1], col_recv.at[0], above).wait_send()
 
     pl.when(has_north)(lambda: row_halo(0).wait_send())
     pl.when(has_south)(lambda: row_halo(1).wait_send())
@@ -619,8 +649,10 @@
         vmem(2, chunks + 1, 8, LANES),
         vmem(2, chunks + 1, 8, LANES),
         vmem(4, rows, tile),
-        dma(3, chunks),
-        dma(7),
+        vmem(2, 8, 3 * LANES),
+        vmem(2, 8, 3 * LANES),
+        dma(chunks),
+        dma(4),
         dma(1),
         dma(chunks),
         dma(1),
@@ -628,10 +660,10 @@
         dma(6),
         dma(4),
         dma(edges),
-        dma(edges),
+        dma(1),
         dma(1),
         dma(2),
-        dma(2, chunks + 1),
+        dma(chunks + 1),
         dma(2),
         dma(2),
         dma(1),

time: 29.8 us -> 29.1 us (0.977)
  the two profiles are of different devices: /device:TPU:1 before, /device:TPU:104 now
where the time goes in v5:
time: 29.1 us; the launch traced here: 28.9 us
  Pallas kernels  28.2 us (97%)
  between operations  0.64 us (2%)
    pallas_call x1, Pallas kernels, shards(): pl.pallas_call(functools.partial(kernel, strips), out_shape=(pltpu.VMEM((...  26.1 us
    pallas_call x1, Pallas kernels, shards(): pl.pallas_call(store_kernel, out_shape=(jax.ShapeDtypeStruct((layers, row...  2.12 us

profile of v5, /device:TPU:104, one launch (start us, length us, event | category | flops | bytes accessed | tf_op | source)
XLA Modules:
  0.0 28.9 jit_solution(1644372005503777860)
XLA Ops:
  0.6 26.1 %soil_column.1 = (f32[8,128,1024]{2,1,0:T(8,128)S(1)}, f32[128,256]{1,0:T(8,128)S(1)}) custom-call(f32[12]{0:T(128)} %ks_hbm.1, f32[12]{0:T(128)} %al_hbm.1, f32[12]{0:T(128)} %th_hbm.1, f32[8,128,1024]{2,1,0:T(8,128)} %p_hbm.1, s32[8,128,1024]{2,1,0:T(8,128)} %t_hbm.1, s32[8,128,1024]{2,1,0:T(8,128)} %a_hbm.1, f32[128,1024]{1,0:T(8,128)} %rain_hbm.1, ...), custom_call_target="tpu_custom_call" | custom-call | tf_op jit(solution)/shard_map/soil_column/pallas_call | solution.py:674
  26.7 2.1 %store.1 = (f32[8,128,1024]{2,1,0:T(8,128)}, f32[128,256]{1,0:T(8,128)}) custom-call(f32[8,128,1024]{2,1,0:T(8,128)S(1)} %get-tuple-element.4.moist, f32[128,256]{1,0:T(8,128)S(1)} %get-tuple-element.5.head), custom_call_target="tpu_custom_call" | custom-call | tf_op jit(solution)/shard_map/store/pallas_call | solution.py:689

commit v6 on v5

--- a/solution.py
+++ b/solution.py
@@ -352,6 +352,10 @@
                 E[q, theirs, cols] = turned(value, 8 - turns[side][n])
             E[2, theirs, cols] = turned(rowrecv[side, :, 2 * LANES :], 8 - turns[side][3 + k])
 
+    def send_pressures(e):
+        pl.when(has_down)(lambda: down_p(e).start())
+        pl.when(has_up)(lambda: up_message(0, e).start())
+
     @pl.loop(0, chunks + 2)
     def _(i):
         @pl.when(i < chunks)
@@ -359,19 +363,24 @@
             three = pl.ds(0, 3 * R)
             pltpu.make_async_copy(p_hbm.at[:, three, :], pbuf.at[:, three, :], load_sem.at[order(i)]).wait()
 
-        @pl.when(i == 0)
+        @pl.when((i == 0) & (x > 0))
         def _():
             pl.semaphore_wait(barrier, greeted)
             announce_first()
 
-        @pl.when(i < EARLY)
-        def _():
-            pl.when(has_down)(lambda: down_p(order(i)).start())
-            pl.when(has_up)(lambda: up_message(0, order(i)).start())
+        @pl.when((i < EARLY) & (i + x > 0))
+        def _():
+            send_pressures(order(i))
 
         @pl.when(i < chunks)
         def _():
             column_pass(order(i))
+
+        @pl.when((i == 0) & start)
+        def _():
+            pl.semaphore_wait(barrier, greeted)
+            announce_first()
+            send_pressures(order(i))
 
         pl.when(i == chunks // 2)(announce_second)
 

time: 29.1 us -> 28.6 us (0.983)
  Pallas kernels: 28.2 us -> 27.8 us
    pallas_call x1, Pallas kernels: 26.1 us -> 25.7 us  [shards(): pl.pallas_call(functools.partial(kernel, strips), out_shape=(pltpu.VMEM((...]
where the time goes in v6:
time: 28.6 us; the launch traced here: 28.5 us
  Pallas kernels  27.8 us (97%)
  between operations  0.64 us (2%)
    pallas_call x1, Pallas kernels, shards(): pl.pallas_call(functools.partial(kernel, strips), out_shape=(pltpu.VMEM((...  25.7 us
    pallas_call x1, Pallas kernels, shards(): pl.pallas_call(store_kernel, out_shape=(jax.ShapeDtypeStruct((layers, row...  2.12 us

profile of v6, /device:TPU:104, one launch (start us, length us, event | category | flops | bytes accessed | tf_op | source)
XLA Modules:
  0.0 28.5 jit_solution(13158564367060423760)
XLA Ops:
  0.6 25.7 %soil_column.1 = (f32[8,128,1024]{2,1,0:T(8,128)S(1)}, f32[128,256]{1,0:T(8,128)S(1)}) custom-call(f32[12]{0:T(128)} %ks_hbm.1, f32[12]{0:T(128)} %al_hbm.1, f32[12]{0:T(128)} %th_hbm.1, f32[8,128,1024]{2,1,0:T(8,128)} %p_hbm.1, s32[8,128,1024]{2,1,0:T(8,128)} %t_hbm.1, s32[8,128,1024]{2,1,0:T(8,128)} %a_hbm.1, f32[128,1024]{1,0:T(8,128)} %rain_hbm.1, ...), custom_call_target="tpu_custom_call" | custom-call | tf_op jit(solution)/shard_map/soil_column/pallas_call | solution.py:683
  26.3 2.1 %store.1 = (f32[8,128,1024]{2,1,0:T(8,128)}, f32[128,256]{1,0:T(8,128)}) custom-call(f32[8,128,1024]{2,1,0:T(8,128)S(1)} %get-tuple-element.4.moist, f32[128,256]{1,0:T(8,128)S(1)} %get-tuple-element.5.head), custom_call_target="tpu_custom_call" | custom-call | tf_op jit(solution)/shard_map/store/pallas_call | solution.py:698

commit v7 on v6

--- a/solution.py
+++ b/solution.py
@@ -180,7 +180,7 @@
 
     def outside(side):
         group = lax.broadcasted_iota(jnp.int32, (8, LANES), 1) // 8
-        for chunk in range(chunks + 1):
+        for chunk in range(colrecv.shape[1]):
             colrecv[side, chunk] = jnp.where(group % 4 == 1, 1.0, 0.0)
 
     pl.when(depth == 0)(lambda: outside(0))
@@ -273,7 +273,6 @@
         E[1, there, mid] = store + river
         E[2, there, mid] = store * old + charge * (leak_rate * layer_thick) + river * sec[here, :]
         E[3, there, mid] = root * old
-        pack(chunk, tiles_of(chunk))
 
     lane = lax.broadcasted_iota(jnp.int32, (8, LANES), 1) // 8
 
@@ -287,7 +286,7 @@
         edge = pl.ds(tile - LANES if side == 0 else 0, LANES)
         out = jnp.zeros((8, LANES), jnp.float32)
         for q in range(4):
-            for h in range(2):
+            for h in range(len(tiles)):
                 group = q + 4 * h
                 shift = (8 * group + (8 if side == 0 else 0)) % LANES
                 value = E[q, tiles[h], edge]
@@ -299,12 +298,14 @@
         return [pl.ds(pl.multiple_of(PAD + chunk * R + 8 * h, 8), 8) for h in range(2)]
 
     halo_tiles = [pl.ds(PAD - 8, 8), pl.ds(PAD + rows_all, 8)]
-
-    def pack(chunk, tiles):
-        pl.when(has_down)(lambda: pack_tiles(0, chunk, tiles))
-        pl.when(has_up)(lambda: pack_tiles(1, chunk, tiles))
-
-    def unpack(chunk, tiles=None):
+    pairs = [tiles_of(chunks - 1) + tiles_of(0), tiles_of(1) + tiles_of(2), tiles_of(3) + tiles_of(4)]
+    pairs += [tiles_of(5), tiles_of(6) + halo_tiles]
+
+    def pack(m):
+        pl.when(has_down)(lambda: pack_tiles(0, m, pairs[m]))
+        pl.when(has_up)(lambda: pack_tiles(1, m, pairs[m]))
+
+    def unpack(chunk):
         pl.when(depth == 0)(lambda: column_halo(1, chunk).wait_recv())
         pl.when(depth == 3)(lambda: column_halo(0, chunk).wait_recv())
 
@@ -316,10 +317,10 @@
 
         west, east = colrecv[0, chunk], colrecv[1, chunk]
         for q in range(4):
-            for h in range(2):
+            for h, there in enumerate(pairs[chunk]):
                 group = q + 4 * h
                 moved = pltpu.roll(west, 120 - 8 * group, 1)
-                E[q, (tiles or tiles_of(chunk))[h], halo] = jnp.where(
+                E[q, there, halo] = jnp.where(
                     lane < 8, pltpu.roll(east, LANES - 8 * group, 1) if group else east, moved
                 )
 
@@ -509,30 +510,31 @@
             pl.when(has_down)(copy)
         post_faces(*up)
 
+    pack(0)
     finish(1)
     finish(2)
+    pack(1)
     finish(3)
     posts([lambda: down_c(0).start()], (0, 2))
     finish(4)
+    pack(2)
     posts([lambda: down_p(EARLY - 1).start()], (2, 3))
     finish(5)
+    pack(3)
     posts([lambda: down_c(1).start()], (3, 4))
     finish(6)
 
     pl.when(has_south)(lambda: take_rows(0))
     pl.when(has_north)(lambda: take_rows(1))
-    pack(chunks, halo_tiles)
+    pack(4)
     posts([lambda e=e: down_p(e).start() for e in range(EARLY, edges - 1)], (4, edges))
     face_step(0)
     face_step(1)
 
-    @pl.loop(0, chunks - 3)
-    def _(chunk):
-        unpack(chunk)
-
-    unpack(chunks - 1)
+    for m in range(4):
+        unpack(m)
     face_step(2)
-    unpack(chunks, halo_tiles)
+    unpack(4)
 
     every = (0, 1, 2, 3)
     wave(0, (0,))
@@ -544,7 +546,6 @@
 
     @pl.loop(5, chunks - 1)
     def _(j):
-        unpack(j)
         wave(j, every)
         hand_on(j - 5)
 
@@ -655,8 +656,8 @@
         vmem(4, rows + 2 * PAD, wide),
         vmem(SWEEPS, rows + 2 * PAD, wide),
         vmem(4, rows + 2 * PAD, wide),
-        vmem(2, chunks + 1, 8, LANES),
-        vmem(2, chunks + 1, 8, LANES),
+        vmem(2, 5, 8, LANES),
+        vmem(2, 5, 8, LANES),
         vmem(4, rows, tile),
         vmem(2, 8, 3 * LANES),
         vmem(2, 8, 3 * LANES),
@@ -672,7 +673,7 @@
         dma(1),
         dma(1),
         dma(2),
-        dma(chunks + 1),
+        dma(5),
         dma(2),
         dma(2),
         dma(1),

time: 28.6 us -> 28.4 us (level)
  no operation moved by 1% of the time
where the time goes in v7:
time: 28.4 us; the launch traced here: 28.2 us
  Pallas kernels  27.6 us (97%)
  between operations  0.64 us (2%)
    pallas_call x1, Pallas kernels, shards(): pl.pallas_call(functools.partial(kernel, strips), out_shape=(pltpu.VMEM((...  25.5 us
    pallas_call x1, Pallas kernels, shards(): pl.pallas_call(store_kernel, out_shape=(jax.ShapeDtypeStruct((layers, row...  2.12 us

profile of v7, /device:TPU:104, one launch (start us, length us, event | category | flops | bytes accessed | tf_op | source)
XLA Modules:
  0.0 28.2 jit_solution(3726622366884446980)
XLA Ops:
  0.6 25.5 %soil_column.1 = (f32[8,128,1024]{2,1,0:T(8,128)S(1)}, f32[128,256]{1,0:T(8,128)S(1)}) custom-call(f32[12]{0:T(128)} %ks_hbm.1, f32[12]{0:T(128)} %al_hbm.1, f32[12]{0:T(128)} %th_hbm.1, f32[8,128,1024]{2,1,0:T(8,128)} %p_hbm.1, s32[8,128,1024]{2,1,0:T(8,128)} %t_hbm.1, s32[8,128,1024]{2,1,0:T(8,128)} %a_hbm.1, f32[128,1024]{1,0:T(8,128)} %rain_hbm.1, ...), custom_call_target="tpu_custom_call" | custom-call | tf_op jit(solution)/shard_map/soil_column/pallas_call | solution.py:684
  26.1 2.1 %store.1 = (f32[8,128,1024]{2,1,0:T(8,128)}, f32[128,256]{1,0:T(8,128)}) custom-call(f32[8,128,1024]{2,1,0:T(8,128)S(1)} %get-tuple-element.4.moist, f32[128,256]{1,0:T(8,128)S(1)} %get-tuple-element.5.head), custom_call_target="tpu_custom_call" | custom-call | tf_op jit(solution)/shard_map/store/pallas_call | solution.py:699
